TPU v7x, 256 devices: a whole 4x4x8 slice. The times are simulated.
256 devices in a mesh: seq: 16 (over y, z_lo), exp: 8 (over x, core), dp: 2 (over z_hi).
Axes of the slice: x: 4, y: 4, z: 8 (z_hi: 2, z_lo: 4; z = z_hi * 4 + z_lo), core: 2. Of those that a mesh axis runs over, the one named last changes fastest.
Arguments:
- queries: bfloat16 [6144, 48, 128], P(('dp', 'seq'), 'exp'), parts along dimension 0, may hold values from -4.5 to 4.5
- keys: bfloat16 [6144, 8, 128], P(('dp', 'seq'), 'exp'), parts along dimension 0, may hold values from -4.5 to 4.5
- values: bfloat16 [6144, 8, 128], P(('dp', 'seq'), 'exp'), parts along dimension 0, may hold values from -16 to 16
- doc_ids: int32 [6144], P('dp'), parts along dimension 0, may hold values from 0 to 2, never falling along the last dimension, each value on 1 to 2560 neighbouring positions
- norm_gain: float32 [6144], replicated, may hold values from 0.1 to 1.9
- expert_ids: int32 [6144, 2], P(('dp', 'seq', 'exp')), parts along dimension 0, may hold values from 0 to 7, all different within a row; in each aligned block of 24 rows (0 to 23, 24 to 47, ...) at most 8 rows name the same one
- route_weights: float32 [6144, 2], P(('dp', 'seq', 'exp')), parts along dimension 0, may hold values from 0.2 to 1
- w_in: bfloat16 [8, 6144, 8192], P('exp', None, 'seq'), may hold values from -0.078125 to 0.078125
- w_out: bfloat16 [8, 8192, 6144], P('exp', 'seq'), may hold values from -0.0625 to 0.0625
Outputs:
- mixed: bfloat16 [6144, 6144], P(('dp', 'seq', 'exp')), parts along dimension 0
There are 2 independent parts, one for each index of `dp`. A program takes and returns all parts, laid end to end along the dimension named above; an argument that names none is the same for every part. Nothing has to cross between parts.
Inputs may be any that keep to these rules, and one draw needn't show every extreme that they name: `doc_ids`: never falling along the sequence. `expert_ids`: within the 24 tokens of one device no expert is named by more than 8 tokens, and in every draw some expert of some device is named by exactly 8; the two experts of a token differ.
All inputs are finite; a program needn't handle non-finite values.
Results may differ from a plain program's by a relative error of at most 0.015.
Values may be sent and summed in bfloat16 or wider, within the bound.
A program may use at most 128 MiB of HBM per device.

v0:
```python
import jax
import jax.numpy as jnp
from jax import lax
from jax.sharding import PartitionSpec as P

WINDOW = 2048


epsilon = 1e-05


def shifted(x, axis, by):
    size = lax.axis_size(axis)
    pairs = [(i, i + by) for i in range(size) if 0 <= i + by < size]
    return lax.ppermute(x, axis, pairs)


def shards(queries, keys, values, doc_ids, norm_gain, expert_ids, route_weights, w_in, w_out):
    block_len, heads_dev, head_dim = queries.shape
    seq_count = lax.axis_size("seq")
    exp_count = lax.axis_size("exp")
    seq_index = lax.axis_index("seq")
    reach_blocks = min(-(-WINDOW // block_len), seq_count - 1)
    own_keys = keys[:, 0, :]
    own_values = values[:, 0, :]
    key_list = [own_keys]
    value_list = [own_values]
    for distance in range(1, reach_blocks + 1):
        far_keys, far_values = shifted((own_keys, own_values), "seq", distance)
        key_list.insert(0, far_keys)
        value_list.insert(0, far_values)
    near_keys = jnp.concatenate(key_list, axis=0)
    near_values = jnp.concatenate(value_list, axis=0)
    key_count = near_keys.shape[0]
    query_rows = jnp.transpose(queries, (1, 0, 2)).reshape(heads_dev * block_len, head_dim)
    score = lax.dot_general(
        query_rows, near_keys, (((1,), (1,)), ((), ())), preferred_element_type=jnp.float32
    )
    score = score * (1.0 / head_dim**0.5)
    query_pos = seq_index * block_len + jnp.arange(block_len, dtype=jnp.int32)
    key_pos = (seq_index - reach_blocks) * block_len + jnp.arange(key_count, dtype=jnp.int32)
    padded_docs = jnp.concatenate(
        [jnp.full((reach_blocks * block_len,), -1, jnp.int32), doc_ids], axis=0
    )
    key_docs = lax.dynamic_slice_in_dim(padded_docs, seq_index * block_len, key_count, 0)
    query_docs = lax.dynamic_slice_in_dim(doc_ids, seq_index * block_len, block_len, 0)
    allowed = (key_pos[None, :] <= query_pos[:, None]) & (
        query_pos[:, None] - key_pos[None, :] < WINDOW
    )
    allowed = allowed & (key_pos[None, :] >= 0) & (query_docs[:, None] == key_docs[None, :])
    allowed = jnp.tile(allowed, (heads_dev, 1))
    score = jnp.where(allowed, score, -jnp.inf)
    top_score = jnp.max(score, axis=1, keepdims=True)
    weights = jnp.where(allowed, jnp.exp(score - top_score), 0.0)
    probs = (weights / jnp.sum(weights, axis=1, keepdims=True)).astype(jnp.bfloat16)
    attended = jnp.dot(probs, near_values, preferred_element_type=jnp.float32).astype(jnp.bfloat16)
    attended = jnp.transpose(attended.reshape(heads_dev, block_len, head_dim), (1, 0, 2)).reshape(
        block_len, heads_dev * head_dim
    )
    attn = lax.all_to_all(attended, "exp", split_axis=0, concat_axis=1, tiled=True)
    token_count = attn.shape[0]
    width = attn.shape[1]
    attn_float = attn.astype(jnp.float32)
    mean_square = jnp.mean(attn_float * attn_float, axis=1, keepdims=True)
    normed = (attn_float * lax.rsqrt(mean_square + epsilon) * norm_gain[None, :]).astype(
        jnp.bfloat16
    )
    capacity = max((token_count + 2) // 3, 2 * token_count // exp_count)
    flat_ids = expert_ids.reshape(token_count * 2)
    onehot = (flat_ids[:, None] == jnp.arange(exp_count, dtype=jnp.int32)[None, :]).astype(
        jnp.int32
    )
    earlier = jnp.cumsum(onehot, axis=0) - onehot
    slot = jnp.sum(earlier * onehot, axis=1)
    local_code = (flat_ids * capacity + slot).reshape(token_count, 2)
    slot_range = jnp.arange(exp_count * capacity, dtype=jnp.int32)
    first_hit = local_code[:, 0:1] == slot_range[None, :]
    second_hit = local_code[:, 1:2] == slot_range[None, :]
    placing = jnp.transpose((first_hit | second_hit).astype(jnp.bfloat16))
    outgoing = jnp.dot(placing, normed, preferred_element_type=jnp.float32).astype(jnp.bfloat16)
    arrived = lax.all_to_all(
        outgoing.reshape(exp_count, capacity, width), "exp", split_axis=0, concat_axis=0, tiled=True
    )
    row_count = exp_count * capacity
    arrived = arrived.reshape(row_count, width)
    weight_in = w_in[0]
    weight_out = w_out[0]
    hidden = jax.nn.silu(
        jnp.dot(
            lax.all_gather(arrived, "seq", axis=0, tiled=True),
            weight_in,
            preferred_element_type=jnp.float32,
        )
    ).astype(jnp.bfloat16)
    summed = lax.psum_scatter(
        jnp.dot(hidden, weight_out, preferred_element_type=jnp.float32).astype(jnp.bfloat16),
        "seq",
        scatter_dimension=0,
        tiled=True,
    )
    expert_out = summed.reshape(exp_count, capacity, width)
    returned = lax.all_to_all(expert_out, "exp", split_axis=0, concat_axis=0, tiled=True).reshape(
        row_count, width
    )
    combine = route_weights[:, 0:1] * first_hit.astype(jnp.float32) + route_weights[
        :, 1:2
    ] * second_hit.astype(jnp.float32)
    moe_part = jnp.dot(
        combine,
        returned.astype(jnp.float32),
        precision=lax.Precision.HIGHEST,
        preferred_element_type=jnp.float32,
    )
    return (attn_float + moe_part).astype(jnp.bfloat16)


def solution(mesh):
    placed = (
        P(("dp", "seq"), "exp", None),
        P(("dp", "seq"), "exp", None),
        P(("dp", "seq"), "exp", None),
        P("dp"),
        P(),
        P(("dp", "seq", "exp"), None),
        P(("dp", "seq", "exp"), None),
        P("exp", None, "seq"),
        P("exp", "seq", None),
    )
    return jax.shard_map(
        shards, mesh=mesh, in_specs=placed, out_specs=P(("dp", "seq", "exp"), None), check_vma=False
    )
```

profile of v0, /device:TPU:1, one launch (start us, length us, event | category | flops | bytes accessed | tf_op | source)
XLA Modules:
  0.0 700.8 jit_solution(10559928560885986458)
XLA Ops:
  6.5 9.8 %collective-permute-start.11 = (bf16[192,128]{1,0:T(8,128)(2,1)}, bf16[192,128]{1,0:T(8,128)(2,1)S(1)}, u32[]{:S(2)}, u32[]{:S(2)}) collective-permute-start(bf16[192,128]{1,0:T(8,128)(2,1)} %bitcast.56), channel_id=1, source_target_pairs={{0,176},{16,192},{32,208},{48,224},{64,240},{1,177},{17,193},{33,2... | collective-permute-start | bytes 147464 | tf_op jit(solution)/shard_map/ppermute | solution.py:15
  20.3 2.3 collective-permute-start.15
  26.8 2.8 copy.21
  29.8 1.3 collective-permute-start.16
  32.4 2.2 collective-permute-start.18
  34.7 5.2 collective-permute-start.19
  41.2 2.8 collective-permute-start.21
  46.8 1.3 collective-permute-start.2
  52.1 4.0 collective-permute-start.6
  57.5 3.9 collective-permute-start.8
  61.4 1.7 collective-permute-start.9
  63.2 2.6 collective-permute-start.10
  66.8 2.0 fusion.34
  68.8 2.9 fusion.2
  71.7 3.0 fusion.9
  76.0 8.8 %all-to-all-start = ((bf16[8,24,768]{2,1,0:T(8,128)(2,1)}), bf16[8,24,768]{2,1,0:T(8,128)(2,1)S(1)}, u32[]{:S(2)}, u32[]{:S(2)}) async-start(bf16[8,24,768]{2,1,0:T(8,128)(2,1)} %all_to_all.16), calls=%async_computation | async-start | bytes 589824 | tf_op jit(solution)/shard_map/all_to_all | solution.py:60
  84.8 6.7 all-to-all-done
  92.3 16.3 %all_to_all.23 = bf16[8,8,6144]{2,1,0:T(8,128)(2,1)} all-to-all(bf16[8,8,6144]{2,1,0:T(8,128)(2,1)S(1)} %fusion.3), channel_id=1, replica_groups=mesh['seq'=16,'exp'=8,'dp'=2] {'exp'}, dimensions={0} | all-to-all | bytes 1572864 | tf_op jit(solution)/shard_map/all_to_all | solution.py:81
  108.9 271.2 %all-gather.2.cloned.1.call-done = bf16[1024,6144]{1,0:T(8,128)(2,1)} async-done(((bf16[64,6144]{1,0:T(8,128)(2,1)}), bf16[1024,6144]{1,0:T(8,128)(2,1)}) %all-gather.2.cloned.1.call-update) | async-done | bytes 12582928 | tf_op jit(solution)/shard_map/all_gather | solution.py:90
  380.2 11.7 %multiply_convert_fusion = bf16[1024,512]{1,0:T(8,128)(2,1)S(1)} fusion(bf16[1024,6144]{1,0:T(8,128)(2,1)} %all-gather.2.cloned.1.call-done, bf16[1,6144,512]{2,1,0:T(8,128)(2,1)} %param.16), kind=kOutput, calls=%fused_computation.16 | convolution fusion | flops 6445072384 | bytes 19922944 | tf_op jit(solution)/shard_map/dot_general | solution.py:89
  391.9 12.5 %convolution_convert_fusion = bf16[1024,6144]{1,0:T(8,128)(2,1)} fusion(bf16[1024,512]{1,0:T(8,128)(2,1)S(1)} %multiply_convert_fusion, bf16[1,512,6144]{2,1,0:T(8,128)(2,1)} %param.17), kind=kOutput, calls=%fused_computation.3 | convolution fusion | flops 6448742400 | bytes 19922944 | tf_op jit(solution)/shard_map/dot_general | solution.py:96
  404.4 270.9 %reduce-scatter.2.cloned.1.call-done = bf16[64,6144]{1,0:T(8,128)(2,1)} async-done(((bf16[1024,6144]{1,0:T(8,128)(2,1)}), bf16[64,6144]{1,0:T(8,128)(2,1)}) %reduce-scatter.2.cloned.1.call-update) | async-done | bytes 786448 | tf_op jit(solution)/shard_map/reduce_scatter | solution.py:95
  675.3 5.3 all-to-all-start.2
  680.6 12.1 %all-to-all-done.2 = bf16[8,8,6144]{2,1,0:T(8,128)(2,1)S(1)} async-done(((bf16[8,8,6144]{2,1,0:T(8,128)(2,1)}), bf16[8,8,6144]{2,1,0:T(8,128)(2,1)S(1)}, u32[]{:S(2)}, u32[]{:S(2)}) %all-to-all-start.2) | async-done | bytes 786464 | tf_op jit(solution)/shard_map/all_to_all | solution.py:102
  (97 shorter events, 23.3 us)
Async XLA Ops:
  6.5 23.2 %collective-permute-start.11 = (bf16[192,128]{1,0:T(8,128)(2,1)}, bf16[192,128]{1,0:T(8,128)(2,1)S(1)}, u32[]{:S(2)}, u32[]{:S(2)}) collective-permute-start(bf16[192,128]{1,0:T(8,128)(2,1)} %bitcast.56), channel_id=1, source_target_pairs={{0,176},{16,192},{32,208},{48,224},{64,240},{1,177},{17,193},{33,2... | collective-permute-start | bytes 147464 | tf_op jit(solution)/shard_map/ppermute | solution.py:15
  16.4 14.7 %collective-permute-start.12 = (bf16[192,128]{1,0:T(8,128)(2,1)}, bf16[192,128]{1,0:T(8,128)(2,1)S(1)}, u32[]{:S(2)}, u32[]{:S(2)}) collective-permute-start(bf16[192,128]{1,0:T(8,128)(2,1)} %bitcast.57), channel_id=1, source_target_pairs={{0,160},{16,176},{32,192},{48,208},{64,224},{80,240},{1,161},{17,1... | collective-permute-start | bytes 147464 | tf_op jit(solution)/shard_map/ppermute | solution.py:15
  17.7 14.8 %collective-permute-start.13 = (bf16[192,128]{1,0:T(8,128)(2,1)}, bf16[192,128]{1,0:T(8,128)(2,1)S(1)}, u32[]{:S(2)}, u32[]{:S(2)}) collective-permute-start(bf16[192,128]{1,0:T(8,128)(2,1)} %bitcast.58), channel_id=1, source_target_pairs={{0,144},{16,160},{32,176},{48,192},{64,208},{80,224},{96,240},{1,1... | collective-permute-start | bytes 147464 | tf_op jit(solution)/shard_map/ppermute | solution.py:15
  19.0 15.7 %collective-permute-start.14 = (bf16[192,128]{1,0:T(8,128)(2,1)}, bf16[192,128]{1,0:T(8,128)(2,1)S(1)}, u32[]{:S(2)}, u32[]{:S(2)}) collective-permute-start(bf16[192,128]{1,0:T(8,128)(2,1)} %bitcast.59), channel_id=1, source_target_pairs={{0,128},{16,144},{32,160},{48,176},{64,192},{80,208},{96,224},{112... | collective-permute-start | bytes 147464 | tf_op jit(solution)/shard_map/ppermute | solution.py:15
  20.3 19.6 %collective-permute-start.15 = (bf16[192,128]{1,0:T(8,128)(2,1)}, bf16[192,128]{1,0:T(8,128)(2,1)S(1)}, u32[]{:S(2)}, u32[]{:S(2)}) collective-permute-start(bf16[192,128]{1,0:T(8,128)(2,1)} %bitcast.60), channel_id=1, source_target_pairs={{0,112},{16,128},{32,144},{48,160},{64,176},{80,192},{96,208},{112... | collective-permute-start | bytes 147464 | tf_op jit(solution)/shard_map/ppermute | solution.py:15
  29.8 11.5 %collective-permute-start.16 = (bf16[192,128]{1,0:T(8,128)(2,1)S(1)}, bf16[192,128]{1,0:T(8,128)(2,1)S(1)}, u32[]{:S(2)}, u32[]{:S(2)}) collective-permute-start(bf16[192,128]{1,0:T(8,128)(2,1)S(1)} %bitcast.61), channel_id=1, source_target_pairs={{0,96},{16,112},{32,128},{48,144},{64,160},{80,176},{96,192},{112,... | collective-permute-start | bytes 147464 | tf_op jit(solution)/shard_map/ppermute | solution.py:15
  31.1 13.0 %collective-permute-start.17 = (bf16[192,128]{1,0:T(8,128)(2,1)S(1)}, bf16[192,128]{1,0:T(8,128)(2,1)S(1)}, u32[]{:S(2)}, u32[]{:S(2)}) collective-permute-start(bf16[192,128]{1,0:T(8,128)(2,1)S(1)} %bitcast.62), channel_id=1, source_target_pairs={{0,80},{16,96},{32,112},{48,128},{64,144},{80,160},{96,176},{112,1... | collective-permute-start | bytes 147464 | tf_op jit(solution)/shard_map/ppermute | solution.py:15
  32.4 13.0 %collective-permute-start.18 = (bf16[192,128]{1,0:T(8,128)(2,1)S(1)}, bf16[192,128]{1,0:T(8,128)(2,1)S(1)}, u32[]{:S(2)}, u32[]{:S(2)}) collective-permute-start(bf16[192,128]{1,0:T(8,128)(2,1)S(1)} %bitcast.63), channel_id=1, source_target_pairs={{0,64},{16,80},{32,96},{48,112},{64,128},{80,144},{96,160},{112,17... | collective-permute-start | bytes 147464 | tf_op jit(solution)/shard_map/ppermute | solution.py:15
  34.7 12.1 %collective-permute-start.19 = (bf16[192,128]{1,0:T(8,128)(2,1)S(1)}, bf16[192,128]{1,0:T(8,128)(2,1)S(1)}, u32[]{:S(2)}, u32[]{:S(2)}) collective-permute-start(bf16[192,128]{1,0:T(8,128)(2,1)S(1)} %bitcast.64), channel_id=1, source_target_pairs={{0,48},{16,64},{32,80},{48,96},{64,112},{80,128},{96,144},{112,160... | collective-permute-start | bytes 147464 | tf_op jit(solution)/shard_map/ppermute | solution.py:15
  39.9 8.2 %collective-permute-start.20 = (bf16[192,128]{1,0:T(8,128)(2,1)S(1)}, bf16[192,128]{1,0:T(8,128)(2,1)S(1)}, u32[]{:S(2)}, u32[]{:S(2)}) collective-permute-start(bf16[192,128]{1,0:T(8,128)(2,1)S(1)} %bitcast.65), channel_id=1, source_target_pairs={{0,32},{16,48},{32,64},{48,80},{64,96},{80,112},{96,128},{112,144}... | collective-permute-start | bytes 147464 | tf_op jit(solution)/shard_map/ppermute | solution.py:15
  41.2 8.2 %collective-permute-start.21 = (bf16[192,128]{1,0:T(8,128)(2,1)S(1)}, bf16[192,128]{1,0:T(8,128)(2,1)S(1)}, u32[]{:S(2)}, u32[]{:S(2)}) collective-permute-start(bf16[192,128]{1,0:T(8,128)(2,1)S(1)} %bitcast.66), channel_id=1, source_target_pairs={{0,16},{16,32},{32,48},{48,64},{64,80},{80,96},{96,112},{112,128},... | collective-permute-start | bytes 147464 | tf_op jit(solution)/shard_map/ppermute | solution.py:15
  44.1 6.6 collective-permute-start
  45.4 6.6 collective-permute-start.1
  46.8 9.4 %collective-permute-start.2 = (bf16[192,128]{1,0:T(8,128)(2,1)S(1)}, bf16[192,128]{1,0:T(8,128)(2,1)S(1)}, u32[]{:S(2)}, u32[]{:S(2)}) collective-permute-start(bf16[192,128]{1,0:T(8,128)(2,1)S(1)} %bitcast.69), channel_id=1, source_target_pairs={{0,144},{16,160},{32,176},{48,192},{64,208},{80,224},{96,240},{1,1... | collective-permute-start | bytes 147464 | tf_op jit(solution)/shard_map/ppermute | solution.py:15
  48.1 9.4 %collective-permute-start.3 = (bf16[192,128]{1,0:T(8,128)(2,1)S(1)}, bf16[192,128]{1,0:T(8,128)(2,1)S(1)}, u32[]{:S(2)}, u32[]{:S(2)}) collective-permute-start(bf16[192,128]{1,0:T(8,128)(2,1)S(1)} %bitcast.70), channel_id=1, source_target_pairs={{0,128},{16,144},{32,160},{48,176},{64,192},{80,208},{96,224},{112... | collective-permute-start | bytes 147464 | tf_op jit(solution)/shard_map/ppermute | solution.py:15
  49.4 12.0 %collective-permute-start.4 = (bf16[192,128]{1,0:T(8,128)(2,1)S(1)}, bf16[192,128]{1,0:T(8,128)(2,1)S(1)}, u32[]{:S(2)}, u32[]{:S(2)}) collective-permute-start(bf16[192,128]{1,0:T(8,128)(2,1)S(1)} %bitcast.71), channel_id=1, source_target_pairs={{0,112},{16,128},{32,144},{48,160},{64,176},{80,192},{96,208},{112... | collective-permute-start | bytes 147464 | tf_op jit(solution)/shard_map/ppermute | solution.py:15
  50.8 12.4 %collective-permute-start.5 = (bf16[192,128]{1,0:T(8,128)(2,1)S(1)}, bf16[192,128]{1,0:T(8,128)(2,1)S(1)}, u32[]{:S(2)}, u32[]{:S(2)}) collective-permute-start(bf16[192,128]{1,0:T(8,128)(2,1)S(1)} %bitcast.72), channel_id=1, source_target_pairs={{0,96},{16,112},{32,128},{48,144},{64,160},{80,176},{96,192},{112,... | collective-permute-start | bytes 147464 | tf_op jit(solution)/shard_map/ppermute | solution.py:15
  52.1 13.7 %collective-permute-start.6 = (bf16[192,128]{1,0:T(8,128)(2,1)S(1)}, bf16[192,128]{1,0:T(8,128)(2,1)S(1)}, u32[]{:S(2)}, u32[]{:S(2)}) collective-permute-start(bf16[192,128]{1,0:T(8,128)(2,1)S(1)} %bitcast.73), channel_id=1, source_target_pairs={{0,80},{16,96},{32,112},{48,128},{64,144},{80,160},{96,176},{112,1... | collective-permute-start | bytes 147464 | tf_op jit(solution)/shard_map/ppermute | solution.py:15
  56.1 9.7 %collective-permute-start.7 = (bf16[192,128]{1,0:T(8,128)(2,1)S(1)}, bf16[192,128]{1,0:T(8,128)(2,1)S(1)}, u32[]{:S(2)}, u32[]{:S(2)}) collective-permute-start(bf16[192,128]{1,0:T(8,128)(2,1)S(1)} %bitcast.74), channel_id=1, source_target_pairs={{0,64},{16,80},{32,96},{48,112},{64,128},{80,144},{96,160},{112,17... | collective-permute-start | bytes 147464 | tf_op jit(solution)/shard_map/ppermute | solution.py:15
  57.5 8.4 %collective-permute-start.8 = (bf16[192,128]{1,0:T(8,128)(2,1)S(1)}, bf16[192,128]{1,0:T(8,128)(2,1)S(1)}, u32[]{:S(2)}, u32[]{:S(2)}) collective-permute-start(bf16[192,128]{1,0:T(8,128)(2,1)S(1)} %bitcast.75), channel_id=1, source_target_pairs={{0,48},{16,64},{32,80},{48,96},{64,112},{80,128},{96,144},{112,160... | collective-permute-start | bytes 147464 | tf_op jit(solution)/shard_map/ppermute | solution.py:15
  76.0 15.5 %all-to-all-start = ((bf16[8,24,768]{2,1,0:T(8,128)(2,1)}), bf16[8,24,768]{2,1,0:T(8,128)(2,1)S(1)}, u32[]{:S(2)}, u32[]{:S(2)}) async-start(bf16[8,24,768]{2,1,0:T(8,128)(2,1)} %all_to_all.16), calls=%async_computation | async-start | bytes 589824 | tf_op jit(solution)/shard_map/all_to_all | solution.py:60
  84.8 295.4 %all-gather.2.cloned.1.call-start = ((), (), s32[]{:S(2)}) async-start(), calls=%async_computation.4 | async-start | bytes 13369344 | tf_op jit(solution)/shard_map/all_gather | solution.py:90
  108.7 566.6 %reduce-scatter.2.cloned.1.call-start = ((), (), s32[]{:S(2)}) async-start(), calls=%async_computation.5 | async-start | bytes 13369344 | tf_op jit(solution)/shard_map/reduce_scatter | solution.py:95
  675.3 17.5 %all-to-all-start.2 = ((bf16[8,8,6144]{2,1,0:T(8,128)(2,1)}), bf16[8,8,6144]{2,1,0:T(8,128)(2,1)S(1)}, u32[]{:S(2)}, u32[]{:S(2)}) async-start(bf16[8,8,6144]{2,1,0:T(8,128)(2,1)} %bitcast.54), calls=%async_computation.3 | async-start | bytes 1572864 | tf_op jit(solution)/shard_map/all_to_all | solution.py:102
  (8 other events, 438.5 us)
Sparse Core Ops, SparseCore 0:
  108.8 271.3 all-gather.1
  404.5 270.7 reduce-scatter.1
where the time goes:
time: 702 us; the launch traced here: 701 us
  waiting for transfers between devices  562 us (80%)
  starting transfers between devices  65.8 us (9%)
  matrix products  30.9 us (4%)
  blocking collectives  16.3 us (2%)
  between operations  14 us (2%)
    all_gather x1, waiting for transfers between devices, shards(): lax.all_gather(arrived, 'seq', axis=0, tiled=True)  271 us
    reduce_scatter x1, waiting for transfers between devices, shards(): lax.psum_scatter(jnp.dot(hidden, weight_out, preferred_element_type=jnp.f...  271 us
    ppermute x22, starting transfers between devices, shifted(): return lax.ppermute(x, axis, pairs)  51.4 us
    all_to_all x1, blocking collectives, shards(): lax.all_to_all(outgoing.reshape(exp_count, capacity, width), 'exp', split...  16.3 us
  transfers between devices with their start and end apart: 26, of which 5 were waited for; matrix products, arithmetic and copies ran while one was open for 1% of the time, Pallas kernels for 0%

commit v1 on v0

--- a/solution.py
+++ b/solution.py
@@ -1,10 +1,19 @@
+import functools
+
 import jax
 import jax.numpy as jnp
 from jax import lax
+from jax.experimental import pallas as pl
+from jax.experimental.pallas import tpu as pltpu
 from jax.sharding import PartitionSpec as P
 
 WINDOW = 2048
-
+EXP = 8
+NY = 4
+NZ = 4
+CAP = 8
+ROWS = EXP * CAP
+HALF = ROWS // 2
 
 epsilon = 1e-05
 
@@ -13,6 +22,245 @@
     size = lax.axis_size(axis)
     pairs = [(i, i + by) for i in range(size) if 0 <= i + by < size]
     return lax.ppermute(x, axis, pairs)
+
+
+def moe_kernel(
+    going, w_in, w_out, result,
+    arrived, rows, hidden, part, halves, sides, quads, leaving, back, wi, wo,
+    w_sem, x_send, x_recv, z_send, z_recv, y_send, y_recv, h_send, h_recv,
+    a_send, a_recv, b_send, b_recv, q_send, q_recv, r_send, r_recv,
+):
+    seq = lax.axis_index("seq")
+    exp = lax.axis_index("exp")
+    y = seq // NZ
+    z = seq % NZ
+    y_up = (y + 1) % NY
+    y_down = (y + NY - 1) % NY
+    y_far = (y + 2) % NY
+    up = {"seq": y_up * NZ + z}
+    down = {"seq": y_down * NZ + z}
+    column = [z, z + 1 - 2 * (z % 2), 2 - z // 2, 3 - 3 * (z // 2)]
+    width = rows.shape[2]
+
+    load_in = pltpu.make_async_copy(w_in, wi, w_sem.at[0])
+    load_out = pltpu.make_async_copy(w_out, wo, w_sem.at[1])
+    load_in.start()
+    load_out.start()
+
+    barrier = pltpu.get_barrier_semaphore()
+    greeted = [up, down]
+    greeted += [{"seq": y * NZ + column[k]} for k in range(1, NZ)]
+    greeted += [{"exp": (exp + d) % EXP} for d in range(1, EXP)]
+    for device in greeted:
+        pl.semaphore_signal(barrier, inc=1, device_id=device, device_id_type=pl.DeviceIdType.MESH)
+    pl.semaphore_wait(barrier, len(greeted))
+
+    sent = []
+
+    def copy(src, dst, send, recv, device):
+        return pltpu.make_async_remote_copy(
+            src_ref=src, dst_ref=dst, send_sem=send, recv_sem=recv,
+            device_id=device, device_id_type=pl.DeviceIdType.MESH,
+        )
+
+    def push(src, dst, send, recv, device):
+        started = copy(src, dst, send, recv, device)
+        started.start()
+        sent.append(started)
+
+    def arrive(dst, send, recv):
+        copy(dst, dst, send, recv, up).wait_recv()
+
+    def block(col, yy):
+        return rows.at[col, pl.ds(pl.multiple_of(yy * ROWS, ROWS), ROWS)]
+
+    def half_block(col, yy, h):
+        return rows.at[col, pl.ds(pl.multiple_of(yy * ROWS + h * HALF, HALF), HALF)]
+
+    def part_block(k, yy):
+        return part.at[k, pl.ds(pl.multiple_of(yy * ROWS, ROWS), ROWS)]
+
+    def part_half(k, yy, h):
+        return part.at[k, pl.ds(pl.multiple_of(yy * ROWS + h * HALF, HALF), HALF)]
+
+    for d in range(1, EXP):
+        other = (exp + d) % EXP
+        push(going.at[other], arrived.at[exp], x_send.at[d - 1], x_recv.at[d - 1], {"exp": other})
+    arrived[exp] = going[exp]
+    for d in range(1, EXP):
+        source = (exp + EXP - d) % EXP
+        arrive(arrived.at[source], x_send.at[d - 1], x_recv.at[d - 1])
+    own_rows = block(z, y)
+    own_rows[...] = arrived[...].reshape(ROWS, width)
+
+    def gather_send(k):
+        if k > 0:
+            arrive(block(column[k], y), z_send.at[k - 1], z_recv.at[column[k]])
+        ref = block(column[k], y)
+        push(ref, ref, y_send.at[k, 0], y_recv.at[k, 0], up)
+        push(ref, ref, y_send.at[k, 1], y_recv.at[k, 1], down)
+
+    def gather_pass(k):
+        arrive(block(column[k], y_down), y_send.at[k, 0], y_recv.at[k, 0])
+        ref = half_block(column[k], y_down, 0)
+        push(ref, ref, h_send.at[k, 0], h_recv.at[k, 0], up)
+        arrive(block(column[k], y_up), y_send.at[k, 1], y_recv.at[k, 1])
+        ref = half_block(column[k], y_up, 1)
+        push(ref, ref, h_send.at[k, 1], h_recv.at[k, 1], down)
+
+    def compute(k):
+        for h in range(2):
+            arrive(half_block(column[k], y_far, h), h_send.at[k, h], h_recv.at[k, h])
+        if k == 0:
+            load_in.wait()
+        rows_now = rows.at[column[k]]
+
+        @pl.loop(0, wi.shape[1] // 256)
+        def _(n):
+            cols = pl.ds(pl.multiple_of(n * 256, 256), 256)
+            v = jnp.dot(rows_now[...], wi[:, cols], preferred_element_type=jnp.float32)
+            hidden[:, cols] = (v / (1.0 + jnp.exp(-v))).astype(jnp.bfloat16)
+
+        if k == 0:
+            load_out.wait()
+
+        @pl.loop(0, width // 512)
+        def _(n):
+            cols = pl.ds(pl.multiple_of(n * 512, 512), 512)
+            part[k, :, cols] = jnp.dot(
+                hidden[...], wo[:, cols], preferred_element_type=jnp.float32
+            ).astype(jnp.bfloat16)
+
+    def reduce_far(k):
+        push(part_half(k, y_far, 0), halves.at[k, 0], a_send.at[k, 0], a_recv.at[k, 0], up)
+        push(part_half(k, y_far, 1), halves.at[k, 1], a_send.at[k, 1], a_recv.at[k, 1], down)
+
+    def reduce_near(k):
+        for h, yy, device in ((0, y_up, up), (1, y_down, down)):
+            arrive(halves.at[k, h], a_send.at[k, h], a_recv.at[k, h])
+            target = part_half(k, yy, h)
+
+            @pl.loop(0, width // 1024)
+            def _(n):
+                cols = pl.ds(pl.multiple_of(n * 1024, 1024), 1024)
+                target[:, cols] = (
+                    target[:, cols].astype(jnp.float32) + halves[k, h, :, cols].astype(jnp.float32)
+                ).astype(jnp.bfloat16)
+
+            push(part_block(k, yy), sides.at[k, h], b_send.at[k, h], b_recv.at[k, h], device)
+
+    def reduce_own(k):
+        for h in range(2):
+            arrive(sides.at[k, h], b_send.at[k, h], b_recv.at[k, h])
+        if k == 0:
+            return
+        target = part_block(k, y)
+
+        @pl.loop(0, width // 512)
+        def _(n):
+            cols = pl.ds(pl.multiple_of(n * 512, 512), 512)
+            target[:, cols] = (
+                target[:, cols].astype(jnp.float32)
+                + sides[k, 0, :, cols].astype(jnp.float32)
+                + sides[k, 1, :, cols].astype(jnp.float32)
+            ).astype(jnp.bfloat16)
+
+        push(target, quads.at[z], q_send.at[k - 1], q_recv.at[z], {"seq": y * NZ + column[k]})
+
+    for k in range(1, NZ):
+        push(own_rows, own_rows, z_send.at[k - 1], z_recv.at[z], {"seq": y * NZ + column[k]})
+    gather_send(0)
+    gather_send(1)
+    gather_pass(0)
+    gather_send(2)
+    gather_pass(1)
+    compute(0)
+    gather_send(3)
+    gather_pass(2)
+    compute(1)
+    reduce_far(1)
+    gather_pass(3)
+    compute(2)
+    reduce_far(2)
+    reduce_near(1)
+    compute(3)
+    reduce_far(3)
+    reduce_near(2)
+    reduce_own(1)
+    reduce_far(0)
+    reduce_near(3)
+    reduce_own(2)
+    reduce_near(0)
+    reduce_own(3)
+    reduce_own(0)
+    for k in range(1, NZ):
+        arrive(quads.at[column[k]], q_send.at[k - 1], q_recv.at[column[k]])
+    mine = part_block(0, y)
+
+    @pl.loop(0, width // 512)
+    def _(n):
+        cols = pl.ds(pl.multiple_of(n * 512, 512), 512)
+        total = (
+            mine[:, cols].astype(jnp.float32)
+            + sides[0, 0, :, cols].astype(jnp.float32)
+            + sides[0, 1, :, cols].astype(jnp.float32)
+        )
+        for k in range(1, NZ):
+            total = total + quads[column[k], :, cols].astype(jnp.float32)
+        leaving[:, :, cols] = total.astype(jnp.bfloat16).reshape(EXP, CAP, 512)
+
+    for d in range(1, EXP):
+        other = (exp + d) % EXP
+        push(leaving.at[other], back.at[exp], r_send.at[d - 1], r_recv.at[d - 1], {"exp": other})
+    back[exp] = leaving[exp]
+    for d in range(1, EXP):
+        source = (exp + EXP - d) % EXP
+        arrive(back.at[source], r_send.at[d - 1], r_recv.at[d - 1])
+    result[...] = back[...].reshape(ROWS, width)
+    for started in sent:
+        started.wait_send()
+
+
+def experts(going, w_in, w_out):
+    width, ff = w_in.shape
+    dma = pltpu.SemaphoreType.DMA
+    b16 = jnp.bfloat16
+    vmem = pltpu.VMEM
+    return pl.pallas_call(
+        moe_kernel,
+        out_shape=jax.ShapeDtypeStruct((ROWS, width), b16),
+        in_specs=[
+            pl.BlockSpec(memory_space=pltpu.VMEM),
+            pl.BlockSpec(memory_space=pl.ANY),
+            pl.BlockSpec(memory_space=pl.ANY),
+        ],
+        out_specs=pl.BlockSpec(memory_space=pltpu.VMEM),
+        scratch_shapes=[
+            vmem((EXP, CAP, width), b16),
+            vmem((NZ, NY * ROWS, width), b16),
+            vmem((NY * ROWS, ff), b16),
+            vmem((NZ, NY * ROWS, width), b16),
+            vmem((NZ, 2, HALF, width), b16),
+            vmem((NZ, 2, ROWS, width), b16),
+            vmem((NZ, ROWS, width), b16),
+            vmem((EXP, CAP, width), b16),
+            vmem((EXP, CAP, width), b16),
+            vmem((width, ff), b16),
+            vmem((ff, width), b16),
+            dma((2,)),
+            dma((EXP - 1,)), dma((EXP - 1,)),
+            dma((NZ - 1,)), dma((NZ,)),
+            dma((NZ, 2)), dma((NZ, 2)),
+            dma((NZ, 2)), dma((NZ, 2)),
+            dma((NZ, 2)), dma((NZ, 2)),
+            dma((NZ, 2)), dma((NZ, 2)),
+            dma((NZ - 1,)), dma((NZ,)),
+            dma((EXP - 1,)), dma((EXP - 1,)),
+        ],
+        compiler_params=pltpu.CompilerParams(
+            collective_id=0, has_side_effects=True, vmem_limit_bytes=67043328
+        ),
+    )(going, w_in, w_out)
 
 
 def shards(queries, keys, values, doc_ids, norm_gain, expert_ids, route_weights, w_in, w_out):
@@ -65,43 +313,19 @@
     normed = (attn_float * lax.rsqrt(mean_square + epsilon) * norm_gain[None, :]).astype(
         jnp.bfloat16
     )
-    capacity = max((token_count + 2) // 3, 2 * token_count // exp_count)
     flat_ids = expert_ids.reshape(token_count * 2)
     onehot = (flat_ids[:, None] == jnp.arange(exp_count, dtype=jnp.int32)[None, :]).astype(
         jnp.int32
     )
     earlier = jnp.cumsum(onehot, axis=0) - onehot
     slot = jnp.sum(earlier * onehot, axis=1)
-    local_code = (flat_ids * capacity + slot).reshape(token_count, 2)
-    slot_range = jnp.arange(exp_count * capacity, dtype=jnp.int32)
+    local_code = (flat_ids * CAP + slot).reshape(token_count, 2)
+    slot_range = jnp.arange(ROWS, dtype=jnp.int32)
     first_hit = local_code[:, 0:1] == slot_range[None, :]
     second_hit = local_code[:, 1:2] == slot_range[None, :]
     placing = jnp.transpose((first_hit | second_hit).astype(jnp.bfloat16))
     outgoing = jnp.dot(placing, normed, preferred_element_type=jnp.float32).astype(jnp.bfloat16)
-    arrived = lax.all_to_all(
-        outgoing.reshape(exp_count, capacity, width), "exp", split_axis=0, concat_axis=0, tiled=True
-    )
-    row_count = exp_count * capacity
-    arrived = arrived.reshape(row_count, width)
-    weight_in = w_in[0]
-    weight_out = w_out[0]
-    hidden = jax.nn.silu(
-        jnp.dot(
-            lax.all_gather(arrived, "seq", axis=0, tiled=True),
-            weight_in,
-            preferred_element_type=jnp.float32,
-        )
-    ).astype(jnp.bfloat16)
-    summed = lax.psum_scatter(
-        jnp.dot(hidden, weight_out, preferred_element_type=jnp.float32).astype(jnp.bfloat16),
-        "seq",
-        scatter_dimension=0,
-        tiled=True,
-    )
-    expert_out = summed.reshape(exp_count, capacity, width)
-    returned = lax.all_to_all(expert_out, "exp", split_axis=0, concat_axis=0, tiled=True).reshape(
-        row_count, width
-    )
+    returned = experts(outgoing.reshape(EXP, CAP, width), w_in[0], w_out[0])
     combine = route_weights[:, 0:1] * first_hit.astype(jnp.float32) + route_weights[
         :, 1:2
     ] * second_hit.astype(jnp.float32)

time: 702 us -> 364 us (0.52)
  waiting for transfers between devices: 562 us -> 7.13 us
  Pallas kernels: 0 us -> 272 us
  matrix products: 30.9 us -> 8.88 us
  blocking collectives: 16.3 us -> 0 us
  between operations: 14 us -> 0.64 us
    pallas_call x0 -> x1, Pallas kernels: none -> 272 us  [experts(): pl.pallas_call(moe_kernel, out_shape=jax.ShapeDtypeStruct((ROWS, width),...]
    all_gather x1 -> x0, waiting for transfers between devices: 271 us -> none  [shards(): lax.all_gather(arrived, 'seq', axis=0, tiled=True)]
    reduce_scatter x1 -> x0, waiting for transfers between devices: 271 us -> none  [shards(): lax.psum_scatter(jnp.dot(hidden, weight_out, preferred_element_type=jnp.f...]
    dot_general x2 -> x0, matrix products: 24.2 us -> none  [the longest x1 12.5 us: shards(): jnp.dot(hidden, weight_out, preferred_element_type=jnp.float32)]
    all_to_all x1 -> x0, blocking collectives: 16.3 us -> none  [shards(): lax.all_to_all(outgoing.reshape(exp_count, capacity, width), 'exp', split...]
    all_to_all x1 -> x0, waiting for transfers between devices: 12.1 us -> none  [shards(): lax.all_to_all(expert_out, 'exp', split_axis=0, concat_axis=0, tiled=True)]
  transfers between devices with their start and end apart: 26 -> 23, of which waited for: 5 -> 2; matrix products, arithmetic and copies ran while one was open for 1% -> 2% of each run, Pallas kernels for 0% -> 0%
where the time goes in v1:
time: 364 us; the launch traced here: 363 us
  Pallas kernels  272 us (75%)
  starting transfers between devices  60.2 us (17%)
  matrix products  8.88 us (2%)
  local copies, waits for them, and re-layouts  8.06 us (2%)
  waiting for transfers between devices  7.13 us (2%)
  other arithmetic  5.62 us (2%)
    pallas_call x1, Pallas kernels, experts(): pl.pallas_call(moe_kernel, out_shape=jax.ShapeDtypeStruct((ROWS, width),...  272 us
    ppermute x22, starting transfers between devices, shifted(): return lax.ppermute(x, axis, pairs)  51.4 us
    all_to_all x1, starting transfers between devices, shards(): lax.all_to_all(attended, 'exp', split_axis=0, concat_axis=1, tiled=True)  8.77 us
  transfers between devices with their start and end apart: 23, of which 2 were waited for; matrix products, arithmetic and copies ran while one was open for 2% of the time, Pallas kernels for 0%

profile of v1, /device:TPU:1, one launch (start us, length us, event | category | flops | bytes accessed | tf_op | source)
XLA Modules:
  0.0 362.8 jit_solution(10119908370312273552)
XLA Ops:
  0.0 9.8 %collective-permute-start.11 = (bf16[192,128]{1,0:T(8,128)(2,1)}, bf16[192,128]{1,0:T(8,128)(2,1)S(1)}, u32[]{:S(2)}, u32[]{:S(2)}) collective-permute-start(bf16[192,128]{1,0:T(8,128)(2,1)} %bitcast.44), channel_id=1, source_target_pairs={{0,176},{16,192},{32,208},{48,224},{64,240},{1,177},{17,193},{33,2... | collective-permute-start | bytes 147464 | tf_op jit(solution)/shard_map/ppermute | solution.py:24
  13.7 2.3 collective-permute-start.15
  21.1 2.8 copy.21
  24.0 1.3 collective-permute-start.16
  25.3 1.3 collective-permute-start.17
  26.6 2.2 collective-permute-start.18
  28.8 5.2 %collective-permute-start.19 = (bf16[192,128]{1,0:T(8,128)(2,1)S(1)}, bf16[192,128]{1,0:T(8,128)(2,1)S(1)}, u32[]{:S(2)}, u32[]{:S(2)}) collective-permute-start(bf16[192,128]{1,0:T(8,128)(2,1)S(1)} %bitcast.52), channel_id=1, source_target_pairs={{0,48},{16,64},{32,80},{48,96},{64,112},{80,128},{96,144},{112,160... | collective-permute-start | bytes 147464 | tf_op jit(solution)/shard_map/ppermute | solution.py:24
  34.1 1.3 collective-permute-start.20
  35.4 2.8 collective-permute-start.21
  39.6 1.3 collective-permute-start.1
  43.6 1.3 collective-permute-start.4
  46.3 4.0 %collective-permute-start.6 = (bf16[192,128]{1,0:T(8,128)(2,1)S(1)}, bf16[192,128]{1,0:T(8,128)(2,1)S(1)}, u32[]{:S(2)}, u32[]{:S(2)}) collective-permute-start(bf16[192,128]{1,0:T(8,128)(2,1)S(1)} %bitcast.61), channel_id=1, source_target_pairs={{0,80},{16,96},{32,112},{48,128},{64,144},{80,160},{96,176},{112,1... | collective-permute-start | bytes 147464 | tf_op jit(solution)/shard_map/ppermute | solution.py:24
  50.3 1.3 collective-permute-start.7
  51.6 3.9 %collective-permute-start.8 = (bf16[192,128]{1,0:T(8,128)(2,1)S(1)}, bf16[192,128]{1,0:T(8,128)(2,1)S(1)}, u32[]{:S(2)}, u32[]{:S(2)}) collective-permute-start(bf16[192,128]{1,0:T(8,128)(2,1)S(1)} %bitcast.63), channel_id=1, source_target_pairs={{0,48},{16,64},{32,80},{48,96},{64,112},{80,128},{96,144},{112,160... | collective-permute-start | bytes 147464 | tf_op jit(solution)/shard_map/ppermute | solution.py:24
  55.6 1.7 collective-permute-start.9
  57.4 2.6 collective-permute-start.10
  61.0 2.0 fusion.28
  63.0 2.9 fusion.2
  65.9 2.9 fusion.6
  70.1 8.8 %all-to-all-start = ((bf16[8,24,768]{2,1,0:T(8,128)(2,1)}), bf16[8,24,768]{2,1,0:T(8,128)(2,1)S(1)}, u32[]{:S(2)}, u32[]{:S(2)}) async-start(bf16[8,24,768]{2,1,0:T(8,128)(2,1)} %all_to_all.10), calls=%async_computation | async-start | bytes 589824 | tf_op jit(solution)/shard_map/all_to_all | solution.py:308
  79.4 6.2 %all-to-all-done = bf16[8,24,768]{2,1,0:T(8,128)(2,1)S(1)} async-done(((bf16[8,24,768]{2,1,0:T(8,128)(2,1)}), bf16[8,24,768]{2,1,0:T(8,128)(2,1)S(1)}, u32[]{:S(2)}, u32[]{:S(2)}) %all-to-all-start) | async-done | bytes 294944 | tf_op jit(solution)/shard_map/all_to_all | solution.py:308
  86.5 1.4 fusion.3.going
  87.9 272.3 %shard_map.91 = bf16[64,6144]{1,0:T(8,128)(2,1)} custom-call(bf16[8,8,6144]{2,1,0:T(8,128)(2,1)} %fusion.3.going, bf16[6144,512]{1,0:T(8,128)(2,1)} %bitcast.37, bf16[512,6144]{1,0:T(8,128)(2,1)} %bitcast.38), custom_call_target="tpu_custom_call" | custom-call | tf_op jit(solution)/shard_map/pallas_call | solution.py:229
  360.3 2.5 fusion.4
  (91 shorter events, 18.0 us)
Async XLA Ops:
  0.0 23.9 %collective-permute-start.11 = (bf16[192,128]{1,0:T(8,128)(2,1)}, bf16[192,128]{1,0:T(8,128)(2,1)S(1)}, u32[]{:S(2)}, u32[]{:S(2)}) collective-permute-start(bf16[192,128]{1,0:T(8,128)(2,1)} %bitcast.44), channel_id=1, source_target_pairs={{0,176},{16,192},{32,208},{48,224},{64,240},{1,177},{17,193},{33,2... | collective-permute-start | bytes 147464 | tf_op jit(solution)/shard_map/ppermute | solution.py:24
  9.8 15.4 %collective-permute-start.12 = (bf16[192,128]{1,0:T(8,128)(2,1)}, bf16[192,128]{1,0:T(8,128)(2,1)S(1)}, u32[]{:S(2)}, u32[]{:S(2)}) collective-permute-start(bf16[192,128]{1,0:T(8,128)(2,1)} %bitcast.45), channel_id=1, source_target_pairs={{0,160},{16,176},{32,192},{48,208},{64,224},{80,240},{1,161},{17,1... | collective-permute-start | bytes 147464 | tf_op jit(solution)/shard_map/ppermute | solution.py:24
  11.1 15.5 %collective-permute-start.13 = (bf16[192,128]{1,0:T(8,128)(2,1)}, bf16[192,128]{1,0:T(8,128)(2,1)S(1)}, u32[]{:S(2)}, u32[]{:S(2)}) collective-permute-start(bf16[192,128]{1,0:T(8,128)(2,1)} %bitcast.46), channel_id=1, source_target_pairs={{0,144},{16,160},{32,176},{48,192},{64,208},{80,224},{96,240},{1,1... | collective-permute-start | bytes 147464 | tf_op jit(solution)/shard_map/ppermute | solution.py:24
  12.4 16.4 %collective-permute-start.14 = (bf16[192,128]{1,0:T(8,128)(2,1)}, bf16[192,128]{1,0:T(8,128)(2,1)S(1)}, u32[]{:S(2)}, u32[]{:S(2)}) collective-permute-start(bf16[192,128]{1,0:T(8,128)(2,1)} %bitcast.47), channel_id=1, source_target_pairs={{0,128},{16,144},{32,160},{48,176},{64,192},{80,208},{96,224},{112... | collective-permute-start | bytes 147464 | tf_op jit(solution)/shard_map/ppermute | solution.py:24
  13.7 20.4 %collective-permute-start.15 = (bf16[192,128]{1,0:T(8,128)(2,1)}, bf16[192,128]{1,0:T(8,128)(2,1)S(1)}, u32[]{:S(2)}, u32[]{:S(2)}) collective-permute-start(bf16[192,128]{1,0:T(8,128)(2,1)} %bitcast.48), channel_id=1, source_target_pairs={{0,112},{16,128},{32,144},{48,160},{64,176},{80,192},{96,208},{112... | collective-permute-start | bytes 147464 | tf_op jit(solution)/shard_map/ppermute | solution.py:24
  20.4 40.6 %copy-start.1 = (bf16[192,6,128]{2,0,1:T(8,128)(2,1)S(1)}, bf16[192,6,128]{2,0,1:T(8,128)(2,1)}, u32[]{:S(2)}) copy-start(bf16[192,6,128]{2,0,1:T(8,128)(2,1)} %param.9) | copy-start | bytes 884740
  24.0 11.5 %collective-permute-start.16 = (bf16[192,128]{1,0:T(8,128)(2,1)S(1)}, bf16[192,128]{1,0:T(8,128)(2,1)S(1)}, u32[]{:S(2)}, u32[]{:S(2)}) collective-permute-start(bf16[192,128]{1,0:T(8,128)(2,1)S(1)} %bitcast.49), channel_id=1, source_target_pairs={{0,96},{16,112},{32,128},{48,144},{64,160},{80,176},{96,192},{112,... | collective-permute-start | bytes 147464 | tf_op jit(solution)/shard_map/ppermute | solution.py:24
  25.3 13.0 %collective-permute-start.17 = (bf16[192,128]{1,0:T(8,128)(2,1)S(1)}, bf16[192,128]{1,0:T(8,128)(2,1)S(1)}, u32[]{:S(2)}, u32[]{:S(2)}) collective-permute-start(bf16[192,128]{1,0:T(8,128)(2,1)S(1)} %bitcast.50), channel_id=1, source_target_pairs={{0,80},{16,96},{32,112},{48,128},{64,144},{80,160},{96,176},{112,1... | collective-permute-start | bytes 147464 | tf_op jit(solution)/shard_map/ppermute | solution.py:24
  26.6 13.0 %collective-permute-start.18 = (bf16[192,128]{1,0:T(8,128)(2,1)S(1)}, bf16[192,128]{1,0:T(8,128)(2,1)S(1)}, u32[]{:S(2)}, u32[]{:S(2)}) collective-permute-start(bf16[192,128]{1,0:T(8,128)(2,1)S(1)} %bitcast.51), channel_id=1, source_target_pairs={{0,64},{16,80},{32,96},{48,112},{64,128},{80,144},{96,160},{112,17... | collective-permute-start | bytes 147464 | tf_op jit(solution)/shard_map/ppermute | solution.py:24
  28.8 12.1 %collective-permute-start.19 = (bf16[192,128]{1,0:T(8,128)(2,1)S(1)}, bf16[192,128]{1,0:T(8,128)(2,1)S(1)}, u32[]{:S(2)}, u32[]{:S(2)}) collective-permute-start(bf16[192,128]{1,0:T(8,128)(2,1)S(1)} %bitcast.52), channel_id=1, source_target_pairs={{0,48},{16,64},{32,80},{48,96},{64,112},{80,128},{96,144},{112,160... | collective-permute-start | bytes 147464 | tf_op jit(solution)/shard_map/ppermute | solution.py:24
  34.1 8.2 %collective-permute-start.20 = (bf16[192,128]{1,0:T(8,128)(2,1)S(1)}, bf16[192,128]{1,0:T(8,128)(2,1)S(1)}, u32[]{:S(2)}, u32[]{:S(2)}) collective-permute-start(bf16[192,128]{1,0:T(8,128)(2,1)S(1)} %bitcast.53), channel_id=1, source_target_pairs={{0,32},{16,48},{32,64},{48,80},{64,96},{80,112},{96,128},{112,144}... | collective-permute-start | bytes 147464 | tf_op jit(solution)/shard_map/ppermute | solution.py:24
  35.4 8.2 %collective-permute-start.21 = (bf16[192,128]{1,0:T(8,128)(2,1)S(1)}, bf16[192,128]{1,0:T(8,128)(2,1)S(1)}, u32[]{:S(2)}, u32[]{:S(2)}) collective-permute-start(bf16[192,128]{1,0:T(8,128)(2,1)S(1)} %bitcast.54), channel_id=1, source_target_pairs={{0,16},{16,32},{32,48},{48,64},{64,80},{80,96},{96,112},{112,128},... | collective-permute-start | bytes 147464 | tf_op jit(solution)/shard_map/ppermute | solution.py:24
  38.3 6.6 %collective-permute-start = (bf16[192,128]{1,0:T(8,128)(2,1)S(1)}, bf16[192,128]{1,0:T(8,128)(2,1)S(1)}, u32[]{:S(2)}, u32[]{:S(2)}) collective-permute-start(bf16[192,128]{1,0:T(8,128)(2,1)S(1)} %bitcast.55), channel_id=1, source_target_pairs={{0,176},{16,192},{32,208},{48,224},{64,240},{1,177},{17,193},{33,2... | collective-permute-start | bytes 147464 | tf_op jit(solution)/shard_map/ppermute | solution.py:24
  39.6 6.6 %collective-permute-start.1 = (bf16[192,128]{1,0:T(8,128)(2,1)S(1)}, bf16[192,128]{1,0:T(8,128)(2,1)S(1)}, u32[]{:S(2)}, u32[]{:S(2)}) collective-permute-start(bf16[192,128]{1,0:T(8,128)(2,1)S(1)} %bitcast.56), channel_id=1, source_target_pairs={{0,160},{16,176},{32,192},{48,208},{64,224},{80,240},{1,161},{17,1... | collective-permute-start | bytes 147464 | tf_op jit(solution)/shard_map/ppermute | solution.py:24
  40.9 9.4 %collective-permute-start.2 = (bf16[192,128]{1,0:T(8,128)(2,1)S(1)}, bf16[192,128]{1,0:T(8,128)(2,1)S(1)}, u32[]{:S(2)}, u32[]{:S(2)}) collective-permute-start(bf16[192,128]{1,0:T(8,128)(2,1)S(1)} %bitcast.57), channel_id=1, source_target_pairs={{0,144},{16,160},{32,176},{48,192},{64,208},{80,224},{96,240},{1,1... | collective-permute-start | bytes 147464 | tf_op jit(solution)/shard_map/ppermute | solution.py:24
  42.3 9.4 %collective-permute-start.3 = (bf16[192,128]{1,0:T(8,128)(2,1)S(1)}, bf16[192,128]{1,0:T(8,128)(2,1)S(1)}, u32[]{:S(2)}, u32[]{:S(2)}) collective-permute-start(bf16[192,128]{1,0:T(8,128)(2,1)S(1)} %bitcast.58), channel_id=1, source_target_pairs={{0,128},{16,144},{32,160},{48,176},{64,192},{80,208},{96,224},{112... | collective-permute-start | bytes 147464 | tf_op jit(solution)/shard_map/ppermute | solution.py:24
  43.6 12.0 %collective-permute-start.4 = (bf16[192,128]{1,0:T(8,128)(2,1)S(1)}, bf16[192,128]{1,0:T(8,128)(2,1)S(1)}, u32[]{:S(2)}, u32[]{:S(2)}) collective-permute-start(bf16[192,128]{1,0:T(8,128)(2,1)S(1)} %bitcast.59), channel_id=1, source_target_pairs={{0,112},{16,128},{32,144},{48,160},{64,176},{80,192},{96,208},{112... | collective-permute-start | bytes 147464 | tf_op jit(solution)/shard_map/ppermute | solution.py:24
  45.0 12.4 %collective-permute-start.5 = (bf16[192,128]{1,0:T(8,128)(2,1)S(1)}, bf16[192,128]{1,0:T(8,128)(2,1)S(1)}, u32[]{:S(2)}, u32[]{:S(2)}) collective-permute-start(bf16[192,128]{1,0:T(8,128)(2,1)S(1)} %bitcast.60), channel_id=1, source_target_pairs={{0,96},{16,112},{32,128},{48,144},{64,160},{80,176},{96,192},{112,... | collective-permute-start | bytes 147464 | tf_op jit(solution)/shard_map/ppermute | solution.py:24
  46.3 13.7 %collective-permute-start.6 = (bf16[192,128]{1,0:T(8,128)(2,1)S(1)}, bf16[192,128]{1,0:T(8,128)(2,1)S(1)}, u32[]{:S(2)}, u32[]{:S(2)}) collective-permute-start(bf16[192,128]{1,0:T(8,128)(2,1)S(1)} %bitcast.61), channel_id=1, source_target_pairs={{0,80},{16,96},{32,112},{48,128},{64,144},{80,160},{96,176},{112,1... | collective-permute-start | bytes 147464 | tf_op jit(solution)/shard_map/ppermute | solution.py:24
  50.3 9.7 %collective-permute-start.7 = (bf16[192,128]{1,0:T(8,128)(2,1)S(1)}, bf16[192,128]{1,0:T(8,128)(2,1)S(1)}, u32[]{:S(2)}, u32[]{:S(2)}) collective-permute-start(bf16[192,128]{1,0:T(8,128)(2,1)S(1)} %bitcast.62), channel_id=1, source_target_pairs={{0,64},{16,80},{32,96},{48,112},{64,128},{80,144},{96,160},{112,17... | collective-permute-start | bytes 147464 | tf_op jit(solution)/shard_map/ppermute | solution.py:24
  51.6 8.4 %collective-permute-start.8 = (bf16[192,128]{1,0:T(8,128)(2,1)S(1)}, bf16[192,128]{1,0:T(8,128)(2,1)S(1)}, u32[]{:S(2)}, u32[]{:S(2)}) collective-permute-start(bf16[192,128]{1,0:T(8,128)(2,1)S(1)} %bitcast.63), channel_id=1, source_target_pairs={{0,48},{16,64},{32,80},{48,96},{64,112},{80,128},{96,144},{112,160... | collective-permute-start | bytes 147464 | tf_op jit(solution)/shard_map/ppermute | solution.py:24
  55.6 4.4 %collective-permute-start.9 = (bf16[192,128]{1,0:T(8,128)(2,1)S(1)}, bf16[192,128]{1,0:T(8,128)(2,1)S(1)}, u32[]{:S(2)}, u32[]{:S(2)}) collective-permute-start(bf16[192,128]{1,0:T(8,128)(2,1)S(1)} %bitcast.64), channel_id=1, source_target_pairs={{0,32},{16,48},{32,64},{48,80},{64,96},{80,112},{96,128},{112,144}... | collective-permute-start | bytes 147464 | tf_op jit(solution)/shard_map/ppermute | solution.py:24
  57.4 3.6 collective-permute-start.10
  70.1 15.5 %all-to-all-start = ((bf16[8,24,768]{2,1,0:T(8,128)(2,1)}), bf16[8,24,768]{2,1,0:T(8,128)(2,1)S(1)}, u32[]{:S(2)}, u32[]{:S(2)}) async-start(bf16[8,24,768]{2,1,0:T(8,128)(2,1)} %all_to_all.10), calls=%async_computation | async-start | bytes 589824 | tf_op jit(solution)/shard_map/all_to_all | solution.py:308
  (7 other events, 114.9 us)

commit v2 on v1

--- a/solution.py
+++ b/solution.py
@@ -18,10 +18,113 @@
 epsilon = 1e-05
 
 
-def shifted(x, axis, by):
-    size = lax.axis_size(axis)
-    pairs = [(i, i + by) for i in range(size) if 0 <= i + by < size]
-    return lax.ppermute(x, axis, pairs)
+def place_on_torus():
+    seq = lax.axis_index("seq")
+    y = seq // NZ
+    z = seq % NZ
+    column = [z, z + 1 - 2 * (z % 2), 2 - z // 2, 3 - 3 * (z // 2)]
+    return y, z, column
+
+
+def context_kernel(
+    keys, values, all_keys, all_values, z_send, z_recv, y_send, y_recv, h_send, h_recv
+):
+    y, z, column = place_on_torus()
+    y_up = (y + 1) % NY
+    y_down = (y + NY - 1) % NY
+    y_far = (y + 2) % NY
+    up = {"seq": y_up * NZ + z}
+    down = {"seq": y_down * NZ + z}
+    length = keys.shape[0]
+    half = length // 2
+
+    barrier = pltpu.get_barrier_semaphore()
+    greeted = [up, down] + [{"seq": y * NZ + column[k]} for k in range(1, NZ)]
+    for device in greeted:
+        pl.semaphore_signal(barrier, inc=1, device_id=device, device_id_type=pl.DeviceIdType.MESH)
+
+    def rows_of(ref, col, yy):
+        start = (yy * NZ + col) * length
+        return ref.at[pl.ds(pl.multiple_of(start, length), length)]
+
+    def half_of(ref, col, yy, h):
+        start = (yy * NZ + col) * length + h * half
+        return ref.at[pl.ds(pl.multiple_of(start, half), half)]
+
+    both = (all_keys, all_values)
+    for own, ref in zip((keys, values), both):
+        rows_of(ref, z, y)[...] = own[...]
+    pl.semaphore_wait(barrier, len(greeted))
+    sent = []
+
+    def copy(ref, send, recv, device):
+        return pltpu.make_async_remote_copy(
+            src_ref=ref, dst_ref=ref, send_sem=send, recv_sem=recv,
+            device_id=device, device_id_type=pl.DeviceIdType.MESH,
+        )
+
+    def push(ref, send, recv, device):
+        started = copy(ref, send, recv, device)
+        started.start()
+        sent.append(started)
+
+    for k in range(1, NZ):
+        for i, ref in enumerate(both):
+            push(
+                rows_of(ref, z, y), z_send.at[k - 1, i], z_recv.at[z, i],
+                {"seq": y * NZ + column[k]},
+            )
+
+    def spread(k):
+        for i, ref in enumerate(both):
+            block = rows_of(ref, column[k], y)
+            if k > 0:
+                copy(block, z_send.at[k - 1, i], z_recv.at[column[k], i], up).wait_recv()
+            push(block, y_send.at[k, 0, i], y_recv.at[k, 0, i], up)
+            push(block, y_send.at[k, 1, i], y_recv.at[k, 1, i], down)
+
+    def pass_on(k):
+        for h, yy, device in ((0, y_down, up), (1, y_up, down)):
+            for i, ref in enumerate(both):
+                block = rows_of(ref, column[k], yy)
+                copy(block, y_send.at[k, h, i], y_recv.at[k, h, i], up).wait_recv()
+                part = half_of(ref, column[k], yy, h)
+                push(part, h_send.at[k, h, i], h_recv.at[k, h, i], device)
+
+    spread(0)
+    spread(1)
+    pass_on(0)
+    spread(2)
+    pass_on(1)
+    spread(3)
+    pass_on(2)
+    pass_on(3)
+    for k in range(NZ):
+        for h in range(2):
+            for i, ref in enumerate(both):
+                part = half_of(ref, column[k], y_far, h)
+                copy(part, h_send.at[k, h, i], h_recv.at[k, h, i], up).wait_recv()
+    for started in sent:
+        started.wait_send()
+
+
+def gather_context(keys, values):
+    length, head_dim = keys.shape
+    dma = pltpu.SemaphoreType.DMA
+    whole = jax.ShapeDtypeStruct((NY * NZ * length, head_dim), keys.dtype)
+    vmem = pl.BlockSpec(memory_space=pltpu.VMEM)
+    return pl.pallas_call(
+        context_kernel,
+        out_shape=(whole, whole),
+        in_specs=[vmem, vmem],
+        out_specs=(vmem, vmem),
+        scratch_shapes=[
+            dma((NZ - 1, 2)), dma((NZ, 2)),
+            dma((NZ, 2, 2)), dma((NZ, 2, 2)),
+            dma((NZ, 2, 2)), dma((NZ, 2, 2)),
+        ],
+        compiler_params=pltpu.CompilerParams(collective_id=1, has_side_effects=True),
+    )(keys, values)
 
 
 def moe_kernel(
@@ -30,16 +133,13 @@
     w_sem, x_send, x_recv, z_send, z_recv, y_send, y_recv, h_send, h_recv,
     a_send, a_recv, b_send, b_recv, q_send, q_recv, r_send, r_recv,
 ):
-    seq = lax.axis_index("seq")
     exp = lax.axis_index("exp")
-    y = seq // NZ
-    z = seq % NZ
+    y, z, column = place_on_torus()
     y_up = (y + 1) % NY
     y_down = (y + NY - 1) % NY
     y_far = (y + 2) % NY
     up = {"seq": y_up * NZ + z}
     down = {"seq": y_down * NZ + z}
-    column = [z, z + 1 - 2 * (z % 2), 2 - z // 2, 3 - 3 * (z // 2)]
     width = rows.shape[2]
 
     load_in = pltpu.make_async_copy(w_in, wi, w_sem.at[0])
@@ -269,33 +369,24 @@
     exp_count = lax.axis_size("exp")
     seq_index = lax.axis_index("seq")
     reach_blocks = min(-(-WINDOW // block_len), seq_count - 1)
-    own_keys = keys[:, 0, :]
-    own_values = values[:, 0, :]
-    key_list = [own_keys]
-    value_list = [own_values]
-    for distance in range(1, reach_blocks + 1):
-        far_keys, far_values = shifted((own_keys, own_values), "seq", distance)
-        key_list.insert(0, far_keys)
-        value_list.insert(0, far_values)
-    near_keys = jnp.concatenate(key_list, axis=0)
-    near_values = jnp.concatenate(value_list, axis=0)
-    key_count = near_keys.shape[0]
+    all_keys, all_values = gather_context(keys[:, 0, :], values[:, 0, :])
+    key_count = (reach_blocks + 1) * block_len
+    key_start = jnp.maximum(seq_index - reach_blocks, 0) * block_len
+    near_keys = lax.dynamic_slice_in_dim(all_keys, key_start, key_count, 0)
+    near_values = lax.dynamic_slice_in_dim(all_values, key_start, key_count, 0)
     query_rows = jnp.transpose(queries, (1, 0, 2)).reshape(heads_dev * block_len, head_dim)
     score = lax.dot_general(
         query_rows, near_keys, (((1,), (1,)), ((), ())), preferred_element_type=jnp.float32
     )
     score = score * (1.0 / head_dim**0.5)
     query_pos = seq_index * block_len + jnp.arange(block_len, dtype=jnp.int32)
-    key_pos = (seq_index - reach_blocks) * block_len + jnp.arange(key_count, dtype=jnp.int32)
-    padded_docs = jnp.concatenate(
-        [jnp.full((reach_blocks * block_len,), -1, jnp.int32), doc_ids], axis=0
-    )
-    key_docs = lax.dynamic_slice_in_dim(padded_docs, seq_index * block_len, key_count, 0)
+    key_pos = key_start + jnp.arange(key_count, dtype=jnp.int32)
+    key_docs = lax.dynamic_slice_in_dim(doc_ids, key_start, key_count, 0)
     query_docs = lax.dynamic_slice_in_dim(doc_ids, seq_index * block_len, block_len, 0)
     allowed = (key_pos[None, :] <= query_pos[:, None]) & (
         query_pos[:, None] - key_pos[None, :] < WINDOW
     )
-    allowed = allowed & (key_pos[None, :] >= 0) & (query_docs[:, None] == key_docs[None, :])
+    allowed = allowed & (query_docs[:, None] == key_docs[None, :])
     allowed = jnp.tile(allowed, (heads_dev, 1))
     score = jnp.where(allowed, score, -jnp.inf)
     top_score = jnp.max(score, axis=1, keepdims=True)

time: 364 us -> 333 us (0.915)
  starting transfers between devices: 60.2 us -> 7.63 us
  Pallas kernels: 272 us -> 298 us
    ppermute x22 -> x0, starting transfers between devices: 51.4 us -> none  [shifted(): return lax.ppermute(x, axis, pairs)]
    pallas_call x0 -> x1, Pallas kernels: none -> 26 us  [gather_context(): pl.pallas_call(context_kernel, out_shape=(whole, whole), in_specs=[vmem,...]
  transfers between devices with their start and end apart: 23 -> 1, of which waited for: 2 -> 1; matrix products, arithmetic and copies ran while one was open for 2% -> 0% of each run, Pallas kernels for 0% -> 0%
where the time goes in v2:
time: 333 us
  Pallas kernels  298 us (89%)
  matrix products  10.1 us (3%)
  local copies, waits for them, and re-layouts  7.99 us (2%)
  starting transfers between devices  7.63 us (2%)
  waiting for transfers between devices  5.46 us (2%)
  other arithmetic  4.06 us (1%)
    pallas_call x1, Pallas kernels, experts(): pl.pallas_call(moe_kernel, out_shape=jax.ShapeDtypeStruct((ROWS, width),...  272 us
    pallas_call x1, Pallas kernels, gather_context(): pl.pallas_call(context_kernel, out_shape=(whole, whole), in_specs=[vmem,...  26 us
    all_to_all x1, starting transfers between devices, shards(): lax.all_to_all(attended, 'exp', split_axis=0, concat_axis=1, tiled=True)  7.63 us
  transfers between devices with their start and end apart: 1, of which 1 were waited for; matrix products, arithmetic and copies ran while one was open for 0% of the time, Pallas kernels for 0%

profile of v2, /device:TPU:1, one launch (start us, length us, event | category | flops | bytes accessed | tf_op | source)
XLA Modules:
  0.0 333.1 jit_solution(3886275133458232730)
XLA Ops:
  0.0 0.8 dynamic_slice.13
  0.8 0.8 dynamic_slice.12
  1.6 0.6 fusion.8
  2.2 0.7 tile.4
  2.9 2.8 copy.21
  5.7 26.0 %shard_map.91 = (bf16[3072,128]{1,0:T(8,128)(2,1)}, bf16[3072,128]{1,0:T(8,128)(2,1)}) custom-call(bf16[192,128]{1,0:T(8,128)(2,1)} %bitcast.40, bf16[192,128]{1,0:T(8,128)(2,1)} %bitcast.41), custom_call_target="tpu_custom_call" | custom-call | tf_op jit(solution)/shard_map/pallas_call | solution.py:116
  31.7 3.0 fusion.31
  34.7 2.9 fusion.2
  37.6 3.2 fusion.6
  40.8 0.2 copy.28
  41.0 1.1 all_to_all.10
  42.1 7.6 %all-to-all-start = ((bf16[8,24,768]{2,1,0:T(8,128)(2,1)}), bf16[8,24,768]{2,1,0:T(8,128)(2,1)S(1)}, u32[]{:S(2)}, u32[]{:S(2)}) async-start(bf16[8,24,768]{2,1,0:T(8,128)(2,1)} %all_to_all.10), calls=%async_computation | async-start | bytes 589824 | tf_op jit(solution)/shard_map/all_to_all | solution.py:399
  49.7 0.1 copy.24
  49.8 0.1 eq.65
  50.1 0.2 select_reduce_fusion
  50.3 0.1 reduce_sum.31
  50.4 0.1 copy.25
  50.5 0.6 slice_bitcast_fusion.2
  51.1 5.5 %all-to-all-done = bf16[8,24,768]{2,1,0:T(8,128)(2,1)S(1)} async-done(((bf16[8,24,768]{2,1,0:T(8,128)(2,1)}), bf16[8,24,768]{2,1,0:T(8,128)(2,1)S(1)}, u32[]{:S(2)}, u32[]{:S(2)}) %all-to-all-start) | async-done | bytes 294944 | tf_op jit(solution)/shard_map/all_to_all | solution.py:399
  56.6 0.2 fusion.9
  56.8 0.6 copy-done
  57.4 1.4 fusion.3.going
  58.8 271.7 %shard_map.92 = bf16[64,6144]{1,0:T(8,128)(2,1)} custom-call(bf16[8,8,6144]{2,1,0:T(8,128)(2,1)} %fusion.3.going, bf16[6144,512]{1,0:T(8,128)(2,1)} %bitcast.33, bf16[512,6144]{1,0:T(8,128)(2,1)} %bitcast.34), custom_call_target="tpu_custom_call" | custom-call | tf_op jit(solution)/shard_map/pallas_call | solution.py:329
  330.5 2.5 fusion.4
  (24 shorter events, 0.3 us)
Async XLA Ops:
  0.0 31.7 %copy-start.1 = (bf16[192,6,128]{2,0,1:T(8,128)(2,1)S(1)}, bf16[192,6,128]{2,0,1:T(8,128)(2,1)}, u32[]{:S(2)}) copy-start(bf16[192,6,128]{2,0,1:T(8,128)(2,1)} %param.9) | copy-start | bytes 884740
  34.7 2.9 copy-start.7
  37.6 12.1 %copy-start.5 = (s32[24,2]{0,1:T(2,128)S(1)}, s32[24,2]{0,1:T(2,128)}, u32[]{:S(2)}) copy-start(s32[24,2]{0,1:T(2,128)} %param.14) | copy-start | bytes 580
  37.6 12.8 %copy-start.6 = (f32[24,2]{0,1:T(2,128)S(1)}, f32[24,2]{0,1:T(2,128)}, u32[]{:S(2)}) copy-start(f32[24,2]{0,1:T(2,128)} %param.15) | copy-start | bytes 580
  37.6 19.8 %copy-start.2 = (f32[6144]{0:T(1024)S(1)}, f32[6144]{0:T(1024)}, u32[]{:S(2)}) copy-start(f32[6144]{0:T(1024)} %param.13) | copy-start | bytes 73732
  42.1 14.4 %all-to-all-start = ((bf16[8,24,768]{2,1,0:T(8,128)(2,1)}), bf16[8,24,768]{2,1,0:T(8,128)(2,1)S(1)}, u32[]{:S(2)}, u32[]{:S(2)}) async-start(bf16[8,24,768]{2,1,0:T(8,128)(2,1)} %all_to_all.10), calls=%async_computation | async-start | bytes 589824 | tf_op jit(solution)/shard_map/all_to_all | solution.py:399
  50.5 8.3 %copy-start.3 = (s32[24]{0:T(128)}, s32[24]{0:T(128)S(1)}, u32[]{:S(2)}) copy-start(s32[24]{0:T(128)S(1)} %get-tuple-element.11) | copy-start | bytes 292
  50.5 8.3 %copy-start.4 = (s32[24]{0:T(128)}, s32[24]{0:T(128)S(1)}, u32[]{:S(2)}) copy-start(s32[24]{0:T(128)S(1)} %get-tuple-element.12) | copy-start | bytes 292
  56.6 0.8 copy-start

commit v3 on v2

v3 whole, which is shorter than its diff:
```python
import functools

import jax
import jax.numpy as jnp
from jax import lax
from jax.experimental import pallas as pl
from jax.experimental.pallas import tpu as pltpu
from jax.sharding import PartitionSpec as P

WINDOW = 2048
EXP = 8
NY = 4
NZ = 4
CAP = 8
ROWS = EXP * CAP
HALF = ROWS // 2
TOK = 24
DIRECT = 3584

epsilon = 1e-05


def place_on_torus():
    seq = lax.axis_index("seq")
    y = seq // NZ
    z = seq % NZ
    column = [z, z + 1 - 2 * (z % 2), 2 - z // 2, 3 - 3 * (z // 2)]
    return y, z, column


def context_kernel(
    keys, values, info, all_keys, all_values, all_info, z_send, z_recv, y_send, y_recv, h_send, h_recv
):
    y, z, column = place_on_torus()
    y_up = (y + 1) % NY
    y_down = (y + NY - 1) % NY
    y_far = (y + 2) % NY
    up = {"seq": y_up * NZ + z}
    down = {"seq": y_down * NZ + z}
    length = {id(ref): own.shape[0] for own, ref in zip((keys, values, info), (all_keys, all_values, all_info))}

    barrier = pltpu.get_barrier_semaphore()
    greeted = [up, down] + [{"seq": y * NZ + column[k]} for k in range(1, NZ)]
    for device in greeted:
        pl.semaphore_signal(barrier, inc=1, device_id=device, device_id_type=pl.DeviceIdType.MESH)

    def rows_of(ref, col, yy):
        size = length[id(ref)]
        return ref.at[pl.ds(pl.multiple_of((yy * NZ + col) * size, size), size)]

    def half_of(ref, col, yy, h):
        size = length[id(ref)]
        half = size // 2
        start = (yy * NZ + col) * size + h * half
        return ref.at[pl.ds(pl.multiple_of(start, half), half)]

    both = (all_keys, all_values, all_info)
    for own, ref in zip((keys, values, info), both):
        rows_of(ref, z, y)[...] = own[...]
    pl.semaphore_wait(barrier, len(greeted))
    sent = []

    def copy(ref, send, recv, device):
        return pltpu.make_async_remote_copy(
            src_ref=ref, dst_ref=ref, send_sem=send, recv_sem=recv,
            device_id=device, device_id_type=pl.DeviceIdType.MESH,
        )

    def push(ref, send, recv, device):
        started = copy(ref, send, recv, device)
        started.start()
        sent.append(started)

    for k in range(1, NZ):
        for i, ref in enumerate(both):
            push(
                rows_of(ref, z, y), z_send.at[k - 1, i], z_recv.at[z, i],
                {"seq": y * NZ + column[k]},
            )

    def spread(k):
        for i, ref in enumerate(both):
            block = rows_of(ref, column[k], y)
            if k > 0:
                copy(block, z_send.at[k - 1, i], z_recv.at[column[k], i], up).wait_recv()
            push(block, y_send.at[k, 0, i], y_recv.at[k, 0, i], up)
            push(block, y_send.at[k, 1, i], y_recv.at[k, 1, i], down)

    def pass_on(k):
        for h, yy, device in ((0, y_down, up), (1, y_up, down)):
            for i, ref in enumerate(both):
                block = rows_of(ref, column[k], yy)
                copy(block, y_send.at[k, h, i], y_recv.at[k, h, i], up).wait_recv()
                part = half_of(ref, column[k], yy, h)
                push(part, h_send.at[k, h, i], h_recv.at[k, h, i], device)

    spread(0)
    spread(1)
    pass_on(0)
    spread(2)
    pass_on(1)
    spread(3)
    pass_on(2)
    pass_on(3)
    for k in range(NZ):
        for h in range(2):
            for i, ref in enumerate(both):
                part = half_of(ref, column[k], y_far, h)
                copy(part, h_send.at[k, h, i], h_recv.at[k, h, i], up).wait_recv()
    for started in sent:
        started.wait_send()


def gather_context(keys, values, info):
    length, head_dim = keys.shape
    dma = pltpu.SemaphoreType.DMA
    whole = jax.ShapeDtypeStruct((NY * NZ * length, head_dim), keys.dtype)
    vmem = pl.BlockSpec(memory_space=pltpu.VMEM)
    return pl.pallas_call(
        context_kernel,
        out_shape=(
            whole, whole, jax.ShapeDtypeStruct((NY * NZ * info.shape[0], info.shape[1]), info.dtype)
        ),
        in_specs=[vmem, vmem, vmem],
        out_specs=(vmem, vmem, vmem),
        scratch_shapes=[
            dma((NZ - 1, 3)), dma((NZ, 3)),
            dma((NZ, 2, 3)), dma((NZ, 2, 3)),
            dma((NZ, 2, 3)), dma((NZ, 2, 3)),
        ],
        compiler_params=pltpu.CompilerParams(collective_id=1, has_side_effects=True),
    )(keys, values, info)


def moe_kernel(
    going, tokens, place, pick, scale, w_in, w_out, result, result_far,
    arrived, rows, hidden, part, halves, sides, quads, leaving, back, wi, wo,
    tok, staged, landed, rows_far, homed, tpart, thalves, tsides, tquads,
    w_sem, x_send, x_recv, z_send, z_recv, y_send, y_recv, h_send, h_recv,
    a_send, a_recv, b_send, b_recv, q_send, q_recv, r_send, r_recv,
    tz_send, tz_recv, ty_send, ty_recv, th_send, th_recv, tx_send, tx_recv,
    tr_send, tr_recv, ta_send, ta_recv, tb_send, tb_recv, tq_send, tq_recv,
):
    exp = lax.axis_index("exp")
    y, z, column = place_on_torus()
    y_up = (y + 1) % NY
    y_down = (y + NY - 1) % NY
    y_far = (y + 2) % NY
    up = {"seq": y_up * NZ + z}
    down = {"seq": y_down * NZ + z}
    near = rows.shape[2]
    far = tok.shape[4]
    f32 = jnp.float32
    b16 = jnp.bfloat16

    load_in = pltpu.make_async_copy(w_in, wi, w_sem.at[0])
    load_out = pltpu.make_async_copy(w_out, wo, w_sem.at[1])
    load_in.start()
    load_out.start()

    barrier = pltpu.get_barrier_semaphore()
    greeted = [up, down]
    greeted += [{"seq": y * NZ + column[k]} for k in range(1, NZ)]
    greeted += [{"exp": (exp + d) % EXP} for d in range(1, EXP)]
    for device in greeted:
        pl.semaphore_signal(barrier, inc=1, device_id=device, device_id_type=pl.DeviceIdType.MESH)
    tok[z, y] = tokens[...]
    pl.semaphore_wait(barrier, len(greeted))

    sent = []

    def copy(src, dst, send, recv, device):
        return pltpu.make_async_remote_copy(
            src_ref=src, dst_ref=dst, send_sem=send, recv_sem=recv,
            device_id=device, device_id_type=pl.DeviceIdType.MESH,
        )

    def push(src, dst, send, recv, device, keep=sent):
        started = copy(src, dst, send, recv, device)
        started.start()
        keep.append(started)

    def arrive(dst, send, recv):
        copy(dst, dst, send, recv, up).wait_recv()

    def tiles(ref, size, body):
        @pl.loop(0, ref.shape[-1] // size)
        def _(n):
            body(pl.ds(pl.multiple_of(n * size, size), size))

    def block(col, yy):
        return rows.at[col, pl.ds(pl.multiple_of(yy * ROWS, ROWS), ROWS)]

    def half_block(col, yy, h):
        return rows.at[col, pl.ds(pl.multiple_of(yy * ROWS + h * HALF, HALF), HALF)]

    def part_block(k, yy):
        return part.at[k, pl.ds(pl.multiple_of(yy * ROWS, ROWS), ROWS)]

    def part_half(k, yy, h):
        return part.at[k, pl.ds(pl.multiple_of(yy * ROWS + h * HALF, HALF), HALF)]

    def far_half(h):
        return pl.ds(h * (far // 2), far // 2)

    def token_send(k):
        ref = tok.at[column[k], y]
        if k > 0:
            arrive(ref, tz_send.at[k - 1], tz_recv.at[column[k]])
        push(ref, ref, ty_send.at[k, 0], ty_recv.at[k, 0], up)
        push(ref, ref, ty_send.at[k, 1], ty_recv.at[k, 1], down)

    def token_pass(k):
        for h, yy, device in ((0, y_down, up), (1, y_up, down)):
            whole = tok.at[column[k], yy]
            arrive(whole, ty_send.at[k, h], ty_recv.at[k, h])
            ref = tok.at[column[k], yy, :, :, far_half(h)]
            push(ref, ref, th_send.at[k, h], th_recv.at[k, h], device)

    stage_sent = [[] for _ in range(NZ)]

    def token_place(k):
        for h in range(2):
            ref = tok.at[column[k], y_far, :, :, far_half(h)]
            arrive(ref, th_send.at[k, h], th_recv.at[k, h])

        @pl.loop(0, NY)
        def _(yy):
            chosen = place[yy * NZ + column[k]]

            def body(cols):
                held = tok[column[k], yy, :, :, cols].astype(f32).reshape(TOK, 512).astype(b16)
                put = jnp.dot(chosen, held, preferred_element_type=f32)
                staged[k, yy, :, :, cols] = put.reshape(EXP, CAP, 512).astype(b16)

            tiles(tok, 512, body)

        for d in range(1, EXP):
            other = (exp + d) % EXP
            push(
                staged.at[k, :, other], landed.at[k, :, exp],
                tx_send.at[k, d - 1], tx_recv.at[k, d - 1], {"exp": other}, stage_sent[k],
            )
        landed[k, :, exp] = staged[k, :, exp]

    for k in range(1, NZ):
        ref = tok.at[z, y]
        push(ref, ref, tz_send.at[k - 1], tz_recv.at[z], {"seq": y * NZ + column[k]})
    token_send(0)

    for d in range(1, EXP):
        other = (exp + d) % EXP
        push(going.at[other], arrived.at[exp], x_send.at[d - 1], x_recv.at[d - 1], {"exp": other})
    arrived[exp] = going[exp]
    token_send(1)
    token_pass(0)
    token_send(2)
    token_pass(1)
    token_send(3)
    token_pass(2)
    token_pass(3)
    for d in range(1, EXP):
        source = (exp + EXP - d) % EXP
        arrive(arrived.at[source], x_send.at[d - 1], x_recv.at[d - 1])
    own_rows = block(z, y)
    own_rows[...] = arrived[...].reshape(ROWS, near)

    def gather_send(k):
        ref = block(column[k], y)
        if k > 0:
            arrive(ref, z_send.at[k - 1], z_recv.at[column[k]])
        push(ref, ref, y_send.at[k, 0], y_recv.at[k, 0], up)
        push(ref, ref, y_send.at[k, 1], y_recv.at[k, 1], down)

    def gather_pass(k):
        for h, yy, device in ((0, y_down, up), (1, y_up, down)):
            arrive(block(column[k], yy), y_send.at[k, h], y_recv.at[k, h])
            ref = half_block(column[k], yy, h)
            push(ref, ref, h_send.at[k, h], h_recv.at[k, h], device)

    def compute(k):
        for d in range(1, EXP):
            source = (exp + EXP - d) % EXP
            arrive(landed.at[k, :, source], tx_send.at[k, d - 1], tx_recv.at[k, d - 1])

        def gather_far(cols):
            rows_far[:, cols] = (
                landed[k, :, :, :, cols].astype(f32).reshape(NY * ROWS, 512).astype(b16)
            )

        tiles(rows_far, 512, gather_far)
        for h in range(2):
            arrive(half_block(column[k], y_far, h), h_send.at[k, h], h_recv.at[k, h])
        if k == 0:
            load_in.wait()
        rows_now = rows.at[column[k]]

        def first(cols):
            v = jnp.dot(rows_now[...], wi[:near, cols], preferred_element_type=f32)
            v = v + jnp.dot(rows_far[...], wi[near:, cols], preferred_element_type=f32)
            hidden[:, cols] = (v / (1.0 + jnp.exp(-v))).astype(b16)

        tiles(hidden, 256, first)
        if k == 0:
            load_out.wait()
        for started in stage_sent[k]:
            started.wait_send()

        @pl.loop(0, far // 512)
        def _(n):
            cols = pl.ds(pl.multiple_of(n * 512, 512), 512)
            wide = pl.ds(pl.multiple_of(near + n * 512, 512), 512)
            out = jnp.dot(hidden[...], wo[:, wide], preferred_element_type=f32)
            staged[k, :, :, :, cols] = out.reshape(NY, EXP, CAP, 512).astype(b16)

        for d in range(1, EXP):
            other = (exp + d) % EXP
            push(
                staged.at[k, :, other], homed.at[k, :, exp],
                tr_send.at[k, d - 1], tr_recv.at[k, d - 1], {"exp": other},
            )
        homed[k, :, exp] = staged[k, :, exp]

        def second(cols):
            part[k, :, cols] = jnp.dot(hidden[...], wo[:, cols], preferred_element_type=f32).astype(b16)

        tiles(part, 512, second)

    def reduce_far(k):
        push(part_half(k, y_far, 0), halves.at[k, 0], a_send.at[k, 0], a_recv.at[k, 0], up)
        push(part_half(k, y_far, 1), halves.at[k, 1], a_send.at[k, 1], a_recv.at[k, 1], down)

    def reduce_near(k):
        for h, yy, device in ((0, y_up, up), (1, y_down, down)):
            arrive(halves.at[k, h], a_send.at[k, h], a_recv.at[k, h])
            target = part_half(k, yy, h)

            def body(cols):
                target[:, cols] = (
                    target[:, cols].astype(f32) + halves[k, h, :, cols].astype(f32)
                ).astype(b16)

            tiles(part, 512, body)
            push(part_block(k, yy), sides.at[k, h], b_send.at[k, h], b_recv.at[k, h], device)

    def reduce_own(k):
        for h in range(2):
            arrive(sides.at[k, h], b_send.at[k, h], b_recv.at[k, h])
        if k == 0:
            return
        target = part_block(k, y)

        def body(cols):
            target[:, cols] = (
                target[:, cols].astype(f32)
                + sides[k, 0, :, cols].astype(f32)
                + sides[k, 1, :, cols].astype(f32)
            ).astype(b16)

        tiles(part, 512, body)
        push(target, quads.at[z], q_send.at[k - 1], q_recv.at[z], {"seq": y * NZ + column[k]})

    def token_mix(k):
        for d in range(1, EXP):
            source = (exp + EXP - d) % EXP
            arrive(homed.at[k, :, source], tr_send.at[k, d - 1], tr_recv.at[k, d - 1])

        @pl.loop(0, NY)
        def _(yy):
            chosen = pick[yy * NZ + column[k]]
            factor = scale[yy * NZ + column[k]]

            def body(cols):
                held = homed[k, yy, :, :, cols].astype(f32).reshape(ROWS, 512).astype(b16)
                got = jnp.dot(chosen, held, preferred_element_type=f32)
                mixed = got[:TOK] * factor[:, 0:1] + got[TOK:] * factor[:, 1:2]
                tpart[k, yy, :, :, cols] = mixed.reshape(TOK // 8, 8, 512).astype(b16)

            tiles(tpart, 512, body)

        for h, device in ((0, up), (1, down)):
            push(
                tpart.at[k, y_far, :, :, far_half(h)], thalves.at[k, h],
                ta_send.at[k, h], ta_recv.at[k, h], device,
            )

    def token_near(k):
        for h, yy, device in ((0, y_up, up), (1, y_down, down)):
            arrive(thalves.at[k, h], ta_send.at[k, h], ta_recv.at[k, h])
            tpart[k, yy, :, :, far_half(h)] = (
                tpart[k, yy, :, :, far_half(h)].astype(f32) + thalves[k, h].astype(f32)
            ).astype(b16)
            push(tpart.at[k, yy], tsides.at[k, h], tb_send.at[k, h], tb_recv.at[k, h], device)

    def token_own(k):
        for h in range(2):
            arrive(tsides.at[k, h], tb_send.at[k, h], tb_recv.at[k, h])
        if k == 0:
            return
        tpart[k, y] = (
            tpart[k, y].astype(f32) + tsides[k, 0].astype(f32) + tsides[k, 1].astype(f32)
        ).astype(b16)
        push(
            tpart.at[k, y], tquads.at[z], tq_send.at[k - 1], tq_recv.at[z],
            {"seq": y * NZ + column[k]},
        )

    for k in range(1, NZ):
        push(own_rows, own_rows, z_send.at[k - 1], z_recv.at[z], {"seq": y * NZ + column[k]})
    gather_send(0)
    for k in range(NZ):
        token_place(k)
    gather_send(1)
    gather_pass(0)
    gather_pass(1)
    gather_send(2)
    compute(0)
    gather_pass(2)
    gather_send(3)
    compute(1)
    reduce_far(1)
    gather_pass(3)
    compute(2)
    reduce_far(2)
    reduce_near(1)
    compute(3)
    reduce_far(3)
    reduce_far(0)
    reduce_near(2)
    reduce_own(1)
    token_mix(0)
    reduce_near(3)
    reduce_near(0)
    token_mix(1)
    reduce_own(2)
    token_near(0)
    token_mix(2)
    token_near(1)
    reduce_own(3)
    token_mix(3)
    token_near(2)
    token_own(0)
    token_own(1)
    reduce_own(0)
    token_near(3)
    token_own(2)
    token_own(3)
    for k in range(1, NZ):
        arrive(quads.at[column[k]], q_send.at[k - 1], q_recv.at[column[k]])
    mine = part_block(0, y)

    def finish(cols):
        total = (
            mine[:, cols].astype(f32)
            + sides[0, 0, :, cols].astype(f32)
            + sides[0, 1, :, cols].astype(f32)
        )
        for k in range(1, NZ):
            total = total + quads[column[k], :, cols].astype(f32)
        leaving[:, :, cols] = total.astype(b16).reshape(EXP, CAP, 512)

    tiles(part, 512, finish)
    for d in range(1, EXP):
        other = (exp + d) % EXP
        push(leaving.at[other], back.at[exp], r_send.at[d - 1], r_recv.at[d - 1], {"exp": other})
    back[exp] = leaving[exp]
    for k in range(1, NZ):
        arrive(tquads.at[column[k]], tq_send.at[k - 1], tq_recv.at[column[k]])
    total = tpart[0, y].astype(f32) + tsides[0, 0].astype(f32) + tsides[0, 1].astype(f32)
    for k in range(1, NZ):
        total = total + tquads[column[k]].astype(f32)
    result_far[...] = total.reshape(TOK, far)
    for d in range(1, EXP):
        source = (exp + EXP - d) % EXP
        arrive(back.at[source], r_send.at[d - 1], r_recv.at[d - 1])
    result[...] = back[...].reshape(ROWS, near)
    for started in sent:
        started.wait_send()


def experts(going, tokens, place, pick, scale, w_in, w_out):
    width, ff = w_in.shape
    near = going.shape[2]
    far = width - near
    dma = pltpu.SemaphoreType.DMA
    b16 = jnp.bfloat16
    vmem = pltpu.VMEM
    inside = pl.BlockSpec(memory_space=pltpu.VMEM)
    outside = pl.BlockSpec(memory_space=pl.ANY)
    wide = (NZ, NY, EXP, CAP, far)
    eights = TOK // 8
    one, each, pair, peers = dma((NZ - 1,)), dma((NZ,)), dma((NZ, 2)), dma((EXP - 1,))
    all_peers = dma((NZ, EXP - 1))
    return pl.pallas_call(
        moe_kernel,
        out_shape=(
            jax.ShapeDtypeStruct((ROWS, near), b16), jax.ShapeDtypeStruct((TOK, far), jnp.float32)
        ),
        in_specs=[inside] * 5 + [outside] * 2,
        out_specs=(inside, inside),
        scratch_shapes=[
            vmem((EXP, CAP, near), b16),
            vmem((NZ, NY * ROWS, near), b16),
            vmem((NY * ROWS, ff), b16),
            vmem((NZ, NY * ROWS, near), b16),
            vmem((NZ, 2, HALF, near), b16),
            vmem((NZ, 2, ROWS, near), b16),
            vmem((NZ, ROWS, near), b16),
            vmem((EXP, CAP, near), b16),
            vmem((EXP, CAP, near), b16),
            vmem((width, ff), b16),
            vmem((ff, width), b16),
            vmem((NZ, NY, eights, 8, far), b16),
            vmem(wide, b16),
            vmem(wide, b16),
            vmem((NY * ROWS, far), b16),
            vmem(wide, b16),
            vmem((NZ, NY, eights, 8, far), b16),
            vmem((NZ, 2, eights, 8, far // 2), b16),
            vmem((NZ, 2, eights, 8, far), b16),
            vmem((NZ, eights, 8, far), b16),
            dma((2,)),
            peers, peers, one, each, pair, pair, pair, pair,
            pair, pair, pair, pair, one, each, peers, peers,
            one, each, pair, pair, pair, pair, all_peers, all_peers,
            all_peers, all_peers, pair, pair, pair, pair, one, each,
        ],
        compiler_params=pltpu.CompilerParams(
            collective_id=0, has_side_effects=True, vmem_limit_bytes=67043328
        ),
    )(going, tokens, place, pick, scale, w_in, w_out)


def shards(queries, keys, values, doc_ids, norm_gain, expert_ids, route_weights, w_in, w_out):
    block_len, heads_dev, head_dim = queries.shape
    seq_count = lax.axis_size("seq")
    exp_count = lax.axis_size("exp")
    seq_index = lax.axis_index("seq")
    reach_blocks = min(-(-WINDOW // block_len), seq_count - 1)
    flat_ids = expert_ids.reshape(TOK * 2)
    onehot = (flat_ids[:, None] == jnp.arange(exp_count, dtype=jnp.int32)[None, :]).astype(
        jnp.int32
    )
    earlier = jnp.cumsum(onehot, axis=0) - onehot
    slot = jnp.sum(earlier * onehot, axis=1)
    local_code = (flat_ids * CAP + slot).reshape(TOK, 2)
    info = jnp.concatenate([local_code.astype(jnp.float32).T, route_weights.T], axis=0)
    info = jnp.pad(info, ((0, 12), (0, 128 - TOK)))
    all_keys, all_values, all_info = gather_context(keys[:, 0, :], values[:, 0, :], info)
    all_info = all_info.reshape(seq_count, 16, 128)[:, :4, :TOK]
    all_codes = all_info[:, :2].astype(jnp.int32)
    slot_range = jnp.arange(ROWS, dtype=jnp.int32)
    hits = (all_codes[:, :, :, None] == slot_range).astype(jnp.bfloat16)
    pick = hits.reshape(seq_count, 2 * TOK, ROWS)
    place = jnp.transpose(hits[:, 0] + hits[:, 1], (0, 2, 1))
    scale = jnp.transpose(all_info[:, 2:], (0, 2, 1))
    key_count = (reach_blocks + 1) * block_len
    key_start = jnp.maximum(seq_index - reach_blocks, 0) * block_len
    near_keys = lax.dynamic_slice_in_dim(all_keys, key_start, key_count, 0)
    near_values = lax.dynamic_slice_in_dim(all_values, key_start, key_count, 0)
    query_rows = jnp.transpose(queries, (1, 0, 2)).reshape(heads_dev * block_len, head_dim)
    score = lax.dot_general(
        query_rows, near_keys, (((1,), (1,)), ((), ())), preferred_element_type=jnp.float32
    )
    score = score * (1.0 / head_dim**0.5)
    query_pos = seq_index * block_len + jnp.arange(block_len, dtype=jnp.int32)
    key_pos = key_start + jnp.arange(key_count, dtype=jnp.int32)
    key_docs = lax.dynamic_slice_in_dim(doc_ids, key_start, key_count, 0)
    query_docs = lax.dynamic_slice_in_dim(doc_ids, seq_index * block_len, block_len, 0)
    allowed = (key_pos[None, :] <= query_pos[:, None]) & (
        query_pos[:, None] - key_pos[None, :] < WINDOW
    )
    allowed = allowed & (query_docs[:, None] == key_docs[None, :])
    allowed = jnp.tile(allowed, (heads_dev, 1))
    score = jnp.where(allowed, score, -jnp.inf)
    top_score = jnp.max(score, axis=1, keepdims=True)
    weights = jnp.where(allowed, jnp.exp(score - top_score), 0.0)
    probs = (weights / jnp.sum(weights, axis=1, keepdims=True)).astype(jnp.bfloat16)
    attended = jnp.dot(probs, near_values, preferred_element_type=jnp.float32).astype(jnp.bfloat16)
    attended = jnp.transpose(attended.reshape(heads_dev, block_len, head_dim), (1, 0, 2)).reshape(
        block_len, heads_dev * head_dim
    )
    attn = lax.all_to_all(attended, "exp", split_axis=0, concat_axis=1, tiled=True)
    token_count = attn.shape[0]
    width = attn.shape[1]
    attn_float = attn.astype(jnp.float32)
    mean_square = jnp.mean(attn_float * attn_float, axis=1, keepdims=True)
    normed = (attn_float * lax.rsqrt(mean_square + epsilon) * norm_gain[None, :]).astype(
        jnp.bfloat16
    )
    first_hit = local_code[:, 0:1] == slot_range[None, :]
    second_hit = local_code[:, 1:2] == slot_range[None, :]
    placing = jnp.transpose((first_hit | second_hit).astype(jnp.bfloat16))
    outgoing = jnp.dot(
        placing, normed[:, :DIRECT], preferred_element_type=jnp.float32
    ).astype(jnp.bfloat16)
    returned, far_part = experts(
        outgoing.reshape(EXP, CAP, DIRECT),
        normed[:, DIRECT:].reshape(TOK // 8, 8, width - DIRECT),
        place, pick, scale, w_in[0], w_out[0],
    )
    combine = route_weights[:, 0:1] * first_hit.astype(jnp.float32) + route_weights[
        :, 1:2
    ] * second_hit.astype(jnp.float32)
    near_part = jnp.dot(
        combine,
        returned.astype(jnp.float32),
        precision=lax.Precision.HIGHEST,
        preferred_element_type=jnp.float32,
    )
    moe_part = jnp.concatenate([near_part, far_part], axis=1)
    return (attn_float + moe_part).astype(jnp.bfloat16)


def solution(mesh):
    placed = (
        P(("dp", "seq"), "exp", None),
        P(("dp", "seq"), "exp", None),
        P(("dp", "seq"), "exp", None),
        P("dp"),
        P(),
        P(("dp", "seq", "exp"), None),
        P(("dp", "seq", "exp"), None),
        P("exp", None, "seq"),
        P("exp", "seq", None),
    )
    return jax.shard_map(
        shards, mesh=mesh, in_specs=placed, out_specs=P(("dp", "seq", "exp"), None), check_vma=False
    )
```

time: 333 us -> 248 us (0.74)
  Pallas kernels: 298 us -> 208 us
  other arithmetic: 4.06 us -> 9.34 us
    pallas_call x2, Pallas kernels: 298 us -> 208 us  [the longest x1 181 us: experts(): pl.pallas_call(moe_kernel, out_shape=(jax.ShapeDtypeStruct((ROWS, near),...]
  transfers between devices with their start and end apart: 1 -> 1, of which waited for: 1 -> 1; matrix products, arithmetic and copies ran while one was open for 0% -> 2% of each run, Pallas kernels for 0% -> 0%
where the time goes in v3:
time: 248 us; the launch traced here: 247 us
  Pallas kernels  208 us (84%)
  local copies, waits for them, and re-layouts  9.59 us (4%)
  other arithmetic  9.34 us (4%)
  matrix products  8.74 us (4%)
  starting transfers between devices  7.64 us (3%)
  waiting for transfers between devices  2.6 us (1%)
    pallas_call x1, Pallas kernels, experts(): pl.pallas_call(moe_kernel, out_shape=(jax.ShapeDtypeStruct((ROWS, near),...  181 us
    pallas_call x1, Pallas kernels, gather_context(): pl.pallas_call(context_kernel, out_shape=(whole, whole, jax.ShapeDtypeStr...  27.3 us
    all_to_all x1, starting transfers between devices, shards(): lax.all_to_all(attended, 'exp', split_axis=0, concat_axis=1, tiled=True)  7.64 us
  transfers between devices with their start and end apart: 1, of which 1 were waited for; matrix products, arithmetic and copies ran while one was open for 2% of the time, Pallas kernels for 0%

profile of v3, /device:TPU:1, one launch (start us, length us, event | category | flops | bytes accessed | tf_op | source)
XLA Modules:
  0.0 246.6 jit_solution(8431918476471579771)
XLA Ops:
  0.0 0.8 dynamic_slice.13
  0.9 0.8 dynamic_slice.12
  1.7 0.6 fusion.7
  2.3 0.7 tile.4
  2.9 2.8 %copy.16 = pred[1152,2304]{0,1:T(32,128)(4,1)S(1)} copy(pred[1152,2304]{1,0:T(32,128)(4,1)S(1)} %bitcast.43) | data formatting | bytes 5308416 | tf_op jit(solution)/shard_map/tile | solution.py:574
  6.5 0.6 select_maximum_fusion.info
  7.1 27.3 %shard_map.91 = (bf16[3072,128]{1,0:T(8,128)(2,1)}, bf16[3072,128]{1,0:T(8,128)(2,1)}, f32[256,128]{1,0:T(8,128)}) custom-call(bf16[192,128]{1,0:T(8,128)(2,1)} %bitcast.52, bf16[192,128]{1,0:T(8,128)(2,1)} %bitcast.53, f32[16,128]{1,0:T(8,128)} %select_maximum_fusion.info), custom_call_target="tpu_custom_call" | custom-call | tf_op jit(solution)/shard_map/pallas_call | solution.py:119
  34.4 3.0 %fusion.35 = (f32[1152]{0:T(1024)S(1)}, f32[1152,2304]{0,1:T(8,128)S(1)}) fusion(pred[1152,2304]{0,1:T(32,128)(4,1)S(1)} %copy.16, bf16[1152,128]{1,0:T(8,128)(2,1)S(1)} %bitcast.51, bf16[3072,128]{1,0:T(8,128)(2,1)} %get-tuple-element.10, s32[]{:T(128)S(6)} %select_n.16), kind=kOutput, calls=%fused_computation.65 | convolution fusion | flops 687438720 | bytes 14160388 | tf_op jit(solution)/shard_map/dot_general | solution.py:562
  37.4 2.9 %fusion.2 = f32[1152]{0:T(1024)S(1)} fusion(pred[1152,2304]{0,1:T(32,128)(4,1)S(1)} %copy.16, f32[1152,2304]{0,1:T(8,128)S(1)} %get-tuple-element.24, f32[1152]{0:T(1024)S(1)} %get-tuple-element.23), kind=kLoop, calls=%fused_computation.5 | loop fusion | flops 7961472 | bytes 13280256 | tf_op jit(solution)/shard_map/reduce_sum | solution.py:578
  40.3 3.2 %fusion.5 = bf16[1152,128]{1,0:T(8,128)(2,1)S(1)} fusion(pred[1152,2304]{0,1:T(32,128)(4,1)S(1)} %copy.16, f32[1152,2304]{0,1:T(8,128)S(1)} %get-tuple-element.24, f32[1152]{0:T(1024)S(1)} %fusion.2, f32[1152]{0:T(1024)S(1)} %get-tuple-element.23, bf16[3072,128]{1,0:T(8,128)(2,1)S(1)} %copy-done.7, s32[]{:T(128)S(6)} %select_n.16), kind=kOutput, calls=%fused_computation.9 | convolution fusion | flops 690241536 | bytes 14172164 | tf_op jit(solution)/shard_map/dot_general | solution.py:579
  43.7 1.1 all_to_all.10
  44.8 7.6 %all-to-all-start = ((bf16[8,24,768]{2,1,0:T(8,128)(2,1)}), bf16[8,24,768]{2,1,0:T(8,128)(2,1)S(1)}, u32[]{:S(2)}, u32[]{:S(2)}) async-start(bf16[8,24,768]{2,1,0:T(8,128)(2,1)} %all_to_all.10), calls=%async_computation | async-start | bytes 589824 | tf_op jit(solution)/shard_map/all_to_all | solution.py:583
  52.4 0.9 fusion.34
  53.4 0.6 slice_bitcast_fusion.3
  54.1 0.9 fusion.13.pick
  55.0 0.8 copy.21
  55.9 0.7 fusion.14.place
  56.6 2.6 %all-to-all-done = bf16[8,24,768]{2,1,0:T(8,128)(2,1)S(1)} async-done(((bf16[8,24,768]{2,1,0:T(8,128)(2,1)}), bf16[8,24,768]{2,1,0:T(8,128)(2,1)S(1)}, u32[]{:S(2)}, u32[]{:S(2)}) %all-to-all-start) | async-done | bytes 294944 | tf_op jit(solution)/shard_map/all_to_all | solution.py:583
  59.5 0.6 copy-done
  60.2 0.7 slice_bitcast_fusion.tokens
  60.9 1.2 fusion.4.going
  62.1 181.2 %shard_map.92 = (bf16[64,3584]{1,0:T(8,128)(2,1)}, f32[24,2560]{1,0:T(8,128)}) custom-call(bf16[8,8,3584]{2,1,0:T(8,128)(2,1)} %fusion.4.going, bf16[3,8,2560]{2,1,0:T(8,128)(2,1)} %slice_bitcast_fusion.tokens, bf16[16,64,24]{2,1,0:T(8,128)(2,1)} %fusion.14.place, bf16[16,48,64]{2,1,0:T(8,128)(2,1)} %fusion.13.pick, f32[16,24,2]{2,1,0:T(8,128)} %bitcast.49, ...), custom_call_target="tpu_custom_call" | custom-call | tf_op jit(solution)/shard_map/pallas_call | solution.py:494
  243.2 1.4 fusion.17
  244.7 1.9 fusion.10
  (35 shorter events, 1.6 us)
Async XLA Ops:
  0.0 5.8 %copy-start.6 = (s32[24,2]{0,1:T(2,128)S(1)}, s32[24,2]{0,1:T(2,128)}, u32[]{:S(2)}) copy-start(s32[24,2]{0,1:T(2,128)} %param.14) | copy-start | bytes 580
  0.0 6.5 %copy-start.5 = (f32[24,2]{0,1:T(2,128)S(1)}, f32[24,2]{0,1:T(2,128)}, u32[]{:S(2)}) copy-start(f32[24,2]{0,1:T(2,128)} %param.15) | copy-start | bytes 580
  0.0 34.4 %copy-start.1 = (bf16[192,6,128]{2,0,1:T(8,128)(2,1)S(1)}, bf16[192,6,128]{2,0,1:T(8,128)(2,1)}, u32[]{:S(2)}) copy-start(bf16[192,6,128]{2,0,1:T(8,128)(2,1)} %param.9) | copy-start | bytes 884740
  37.4 2.9 %copy-start.7 = (bf16[3072,128]{1,0:T(8,128)(2,1)S(1)}, bf16[3072,128]{1,0:T(8,128)(2,1)}, u32[]{:S(2)}) copy-start(bf16[3072,128]{1,0:T(8,128)(2,1)} %get-tuple-element.11) | copy-start | bytes 2359300
  40.3 19.8 %copy-start.2 = (f32[6144]{0:T(1024)S(1)}, f32[6144]{0:T(1024)}, u32[]{:S(2)}) copy-start(f32[6144]{0:T(1024)} %param.13) | copy-start | bytes 73732
  44.8 14.4 %all-to-all-start = ((bf16[8,24,768]{2,1,0:T(8,128)(2,1)}), bf16[8,24,768]{2,1,0:T(8,128)(2,1)S(1)}, u32[]{:S(2)}, u32[]{:S(2)}) async-start(bf16[8,24,768]{2,1,0:T(8,128)(2,1)} %all_to_all.10), calls=%async_computation | async-start | bytes 589824 | tf_op jit(solution)/shard_map/all_to_all | solution.py:583
  55.0 7.1 %copy-start.3 = (s32[24]{0:T(128)}, s32[24]{0:T(128)S(1)}, u32[]{:S(2)}) copy-start(s32[24]{0:T(128)S(1)} %get-tuple-element.21) | copy-start | bytes 292
  55.0 7.1 %copy-start.4 = (s32[24]{0:T(128)}, s32[24]{0:T(128)S(1)}, u32[]{:S(2)}) copy-start(s32[24]{0:T(128)S(1)} %get-tuple-element.22) | copy-start | bytes 292
  59.3 0.8 copy-start
